TPU v7x, 256 devices: a whole 4x4x8 slice. The times are simulated.
256 devices in a mesh: tm: 32 (over x, y, core), space: 8 (over z).
Axes of the slice: x: 4, y: 4, z: 8, core: 2. Of those that a mesh axis runs over, the one named last changes fastest.
Arguments:
- starts: float32 [32, 128, 16, 256], P('tm', 'space'), may hold values from -6 to 6
- east_velocity: float32 [128, 16, 256], P('space'), may hold values from -0.3 to 0.3
- vertical_velocity: float32 [128, 16, 256], P('space'), may hold values from -0.05 to 0.05
- north_velocity: float32 [128, 16, 256], P('space'), may hold values from -0.1 to 0.1
- class_map: int32 [128, 16, 256], P('space'), may hold values from 0 to 7
- land_mask: int32 [128, 16, 256], P('space'), may hold values 0 or 1
- class_diffusivity: float32 [8], replicated, may hold values from 0.005 to 0.08
Outputs:
- new_ends: float32 [32, 128, 16, 256], P('tm', 'space')
All inputs are finite; a program needn't handle non-finite values. No bound on the sum of `land_mask` on one device may be relied on, other than what follows from the above.
Results may differ from a plain program's by a relative error of at most 0.00002.
Values sent between devices are 32-bit elements; how exact they have to be, the bound alone decides.
A program may use at most 192 MiB of HBM per device.

v0:
```python
import jax
import jax.numpy as jnp
from jax import lax
from jax.sharding import PartitionSpec as P

FINE = 8
COARSE = 4


def padded_2(block, sides, width):
    for axis, dim in sides:
        count = lax.axis_size(axis)
        forward = [(i, i + 1) for i in range(count - 1)]
        backward = [(target, source) for source, target in forward]
        low = lax.ppermute(
            lax.slice_in_dim(block, block.shape[dim] - width, None, axis=dim), axis, forward
        )
        high = lax.ppermute(lax.slice_in_dim(block, 0, width, axis=dim), axis, backward)
        block = jnp.concatenate([low, block, high], axis=dim)
    return block


def shifted(block, axis, distance):
    devices = range(lax.axis_size(axis))
    route = [(i - distance, i) for i in devices if i - distance in devices]
    return lax.ppermute(block, axis, route)


def lower_part(array, direction):
    return lax.slice_in_dim(array, 0, array.shape[direction] - 1, axis=direction)


def upper_part(array, direction):
    return lax.slice_in_dim(array, 1, array.shape[direction], axis=direction)


def advance(tracer, statics, mix_scale):
    diffusivity = statics[3]
    openness = statics[4]
    change = jnp.zeros_like(tracer)
    for direction in range(3):
        speed = statics[direction]
        open_face = lower_part(openness, direction) * upper_part(openness, direction)
        face_speed = 0.5 * (lower_part(speed, direction) + upper_part(speed, direction)) * open_face
        face_mix = (
            mix_scale
            * 0.5
            * (lower_part(diffusivity, direction) + upper_part(diffusivity, direction))
            * open_face
        )
        left_value = lower_part(tracer, direction)
        right_value = upper_part(tracer, direction)
        flux = (
            jnp.maximum(face_speed, 0.0) * left_value
            + jnp.minimum(face_speed, 0.0) * right_value
            + face_mix * (left_value - right_value)
        )
        pad_widths = [(0, 0), (0, 0), (0, 0)]
        pad_widths[direction] = (1, 1)
        padded_flux = jnp.pad(flux, pad_widths)
        change = change + (upper_part(padded_flux, direction) - lower_part(padded_flux, direction))
    return tracer - change


def restrict(array):
    shape = array.shape
    leading = shape[:-3]
    lead_rank = len(leading)
    reshaped = array.reshape(leading + (shape[-3] // 2, 2, shape[-2] // 2, 2, shape[-1] // 2, 2))
    return jnp.mean(reshaped, axis=(lead_rank + 1, lead_rank + 3, lead_rank + 5))


def prolong(array):
    return jnp.repeat(jnp.repeat(jnp.repeat(array, 2, axis=-3), 2, axis=-2), 2, axis=-1)


def build_statics(
    east_velocity, vertical_velocity, north_velocity, class_map, land_mask, class_diffusivity
):
    classes = jnp.arange(class_diffusivity.shape[0], dtype=jnp.int32)
    diffusivity = jnp.sum(
        jnp.where(
            class_map[None] == classes[:, None, None, None],
            class_diffusivity[:, None, None, None],
            0.0,
        ),
        axis=0,
    )
    return jnp.stack(
        [
            east_velocity,
            vertical_velocity,
            north_velocity,
            diffusivity,
            land_mask.astype(jnp.float32),
        ]
    )


def shards(
    starts,
    east_velocity,
    vertical_velocity,
    north_velocity,
    class_map,
    land_mask,
    class_diffusivity,
):
    slab_width = starts.shape[1]
    statics = build_statics(
        east_velocity, vertical_velocity, north_velocity, class_map, land_mask, class_diffusivity
    )
    band_depth = 1
    wide_statics = padded_2(statics, (("space", 1),), FINE)
    coarse_statics = restrict(wide_statics)
    statics_band = wide_statics[:, FINE - band_depth : FINE + slab_width + band_depth]
    tracer = starts[0]
    for substep in range(FINE):
        padded = padded_2(tracer, (("space", 0),), 1)
        tracer = advance(padded, statics_band, 1.0)[1:-1]

    def coarse_prop(coarse_state):
        padded_state = padded_2(coarse_state, (("space", 0),), COARSE)
        for substep in range(COARSE):
            padded_state = advance(padded_state, coarse_statics, 0.5)
        return padded_state[COARSE:-COARSE]

    own_coarse = restrict(starts[0])
    first_guess = coarse_prop(own_coarse)
    defect = restrict(tracer) - first_guess
    position = lax.axis_index("tm")
    slices = lax.axis_size("tm")

    def pass_turn(turn_index, current):
        arrived = shifted(current + defect, "tm", 1)
        return coarse_prop(jnp.where(position == 0, own_coarse, arrived))

    latest = lax.fori_loop(0, slices - 1, pass_turn, first_guess)
    result = tracer + prolong(latest - first_guess)
    return result[None]


def solution(mesh):
    in_specs = (
        P("tm", "space", None, None),
        P("space", None, None),
        P("space", None, None),
        P("space", None, None),
        P("space", None, None),
        P("space", None, None),
        P(),
    )
    out_specs = P("tm", "space", None, None)
    return jax.shard_map(shards, mesh=mesh, in_specs=in_specs, out_specs=out_specs, check_vma=False)
```

profile of v0, /device:TPU:130, one launch (start us, length us, event | category | flops | bytes accessed | tf_op | source)
XLA Modules:
  0.0 831.3 jit_solution(13685886815528114914)
XLA Ops:
  11.4 18.1 %reshape_squeeze.3 = f32[8,2,8,2,128,2]{5,4,3,2,1,0:T(8,128)} reshape(f32[1,16,16,256]{3,2,1,0:T(8,128)S(1)} %copy-done.2) | data formatting | bytes 524288 | tf_op jit(solution)/shard_map/reshape;squeeze | solution.py:69
  29.5 7.0 reduce_sum.37
  42.3 4.4 collective-permute-start.4
  49.6 4.1 collective-permute-done.3
  58.0 32.1 %copy.1179 = f32[5,32,16,256]{0,3,2,1:T(8,128)} copy(f32[5,32,16,256]{3,2,1,0:T(8,128)S(1)} %pad_maximum_fusion.1) | data formatting | bytes 5242880 | tf_op jit(solution)/shard_map/concatenate | solution.py:19
  90.1 46.6 %reduce_sum.38 = f32[5,16,8,128]{0,3,2,1:T(8,128)} reduce(f32[5,16,2,8,2,128,2]{0,6,5,4,3,2,1:T(2,128)} %bitcast.15, f32[]{:T(128)} %constant.29.clone.1), dimensions={2,4,6}, to_apply=%region_2.3 | reduce | flops 573440 | bytes 2949124 | tf_op jit(solution)/shard_map/reduce_sum | solution.py:70
  136.7 8.3 broadcast_multiply_fusion
  145.0 28.4 %slice_reduce_fusion = (f32[16,8,128]{2,1,0:T(8,128)S(1)}, f32[16,8,128]{2,1,0:T(8,128)S(1)}, f32[16,8,128]{2,1,0:T(8,128)S(1)}, f32[16,8,128]{2,1,0:T(8,128)S(1)}) fusion(f32[5,16,8,128]{0,3,2,1:T(8,128)} %broadcast_multiply_fusion), kind=kLoop, calls=%fused_computation.68 | loop fusion | bytes 524288 | tf_op jit(solution)/shard_map/slice | solution.py:42
  173.5 26.6 %fusion.22 = (f32[15,8,128]{2,1,0:T(8,128)S(1)}, f32[15,8,128]{2,1,0:T(8,128)S(1)}, f32[15,8,128]{2,1,0:T(8,128)S(1)}) fusion(f32[5,16,8,128]{0,3,2,1:T(8,128)} %broadcast_multiply_fusion), kind=kLoop, calls=%fused_computation.77 | loop fusion | flops 46080 | bytes 552960 | tf_op jit(solution)/shard_map/add | solution.py:44
  205.6 3.9 collective-permute-start.7
  215.0 3.9 collective-permute-start.9
  224.4 3.9 collective-permute-start.11
  233.7 3.9 collective-permute-start.13
  243.1 3.9 collective-permute-start.15
  252.5 3.9 collective-permute-start.17
  261.9 3.9 collective-permute-start.19
  269.6 18.3 %reshape.66 = f32[8,2,8,2,128,2]{5,4,3,2,1,0:T(8,128)} reshape(f32[16,16,256]{2,1,0:T(8,128)S(1)} %slice_subtract_fusion.4) | data formatting | bytes 524288 | tf_op jit(solution)/shard_map/reshape | solution.py:69
  287.9 7.0 reduce_sum.39
  295.0 533.8 %while.12 = (s32[]{:T(128)}, f32[8,8,128]{2,1,0:T(8,128)S(1)}, pred[]{:T(512)}, f32[8,8,128]{2,1,0:T(8,128)S(1)}, f32[8,8,128]{2,1,0:T(8,128)S(1)}, /*index=5*/f...) while((s32[]{:T(128)}, f32[8,8,128]{2,1,0:T(8,128)S(1)}, ...), condition=%wide.region_5.6_spmd, body=%wide.region_4.5_spmd.sunk | while | flops 2080258 | bytes 6667014 | solution.py:138
  297.0 5.4 collective-permute-done
  304.4 3.9 collective-permute-start.2
  314.2 5.4 collective-permute-done
  321.6 3.9 collective-permute-start.2
  331.4 5.4 collective-permute-done
  338.8 3.9 collective-permute-start.2
  348.7 5.4 collective-permute-done
  356.0 3.9 collective-permute-start.2
  365.9 5.4 collective-permute-done
  373.2 3.9 collective-permute-start.2
  383.1 5.4 collective-permute-done
  390.5 3.9 collective-permute-start.2
  400.3 5.4 collective-permute-done
  407.7 3.9 collective-permute-start.2
  417.5 5.4 collective-permute-done
  424.9 3.9 collective-permute-start.2
  434.7 5.4 collective-permute-done
  452.0 5.4 collective-permute-done
  469.2 5.4 collective-permute-done
  486.4 5.4 collective-permute-done
  493.8 3.9 collective-permute-start.2
  503.6 5.4 collective-permute-done
  520.8 5.4 collective-permute-done
  538.1 5.4 collective-permute-done
  555.3 5.4 collective-permute-done
  562.6 3.9 collective-permute-start.2
  572.5 5.4 collective-permute-done
  589.7 5.4 collective-permute-done
  606.9 5.4 collective-permute-done
  624.1 5.4 collective-permute-done
  631.5 3.9 collective-permute-start.2
  641.4 5.4 collective-permute-done
  658.6 5.4 collective-permute-done
  675.8 5.4 collective-permute-done
  693.0 5.4 collective-permute-done
  700.4 3.9 collective-permute-start.2
  710.2 5.4 collective-permute-done
  727.5 5.4 collective-permute-done
  744.7 5.4 collective-permute-done
  752.0 3.9 collective-permute-start.2
  761.9 5.4 collective-permute-done
  779.1 5.4 collective-permute-done
  796.3 5.4 collective-permute-done
  813.5 5.4 collective-permute-done
  820.9 3.9 collective-permute-start.2
  (990 shorter events, 374.6 us)
Async XLA Ops:
  5.5 48.2 %collective-permute-start.6 = (f32[5,8,16,256]{3,2,1,0:T(8,128)S(1)}, f32[5,8,16,256]{3,2,1,0:T(8,128)S(1)}, u32[]{:S(2)}, u32[]{:S(2)}) collective-permute-start(f32[5,8,16,256]{3,2,1,0:T(8,128)S(1)} %get-tuple-element.212), channel_id=1, source_target_pairs={{1,0},{2,1},{3,2},{4,3},{5,4},{6,5},{7,6},{9,8},{10,9},{11,10},{12... | collective-permute-start | bytes 1966088 | tf_op jit(solution)/shard_map/ppermute | solution.py:18
  7.5 47.6 %collective-permute-start.5 = (f32[5,8,16,256]{3,2,1,0:T(8,128)S(1)}, f32[5,8,16,256]{3,2,1,0:T(8,128)}, u32[]{:S(2)}, u32[]{:S(2)}) collective-permute-start(f32[5,8,16,256]{3,2,1,0:T(8,128)S(1)} %get-tuple-element.211), channel_id=1, source_target_pairs={{0,1},{1,2},{2,3},{3,4},{4,5},{5,6},{6,7},{8,9},{9,10},{10,11},{11... | collective-permute-start | bytes 1966088 | tf_op jit(solution)/shard_map/ppermute | solution.py:15
  36.5 10.3 %collective-permute-start.22 = (f32[4,8,128]{2,1,0:T(8,128)S(1)}, f32[4,8,128]{2,1,0:T(8,128)S(1)}, u32[]{:S(2)}, u32[]{:S(2)}) collective-permute-start(f32[4,8,128]{2,1,0:T(8,128)S(1)} %get-tuple-element.242), channel_id=1, source_target_pairs={{1,0},{2,1},{3,2},{4,3},{5,4},{6,5},{7,6},{9,8},{10,9},{11,10},{12... | collective-permute-start | bytes 49160 | tf_op jit(solution)/shard_map/ppermute | solution.py:18
  39.7 9.2 %collective-permute-start.21 = (f32[4,8,128]{2,1,0:T(8,128)S(1)}, f32[4,8,128]{2,1,0:T(8,128)S(1)}, u32[]{:S(2)}, u32[]{:S(2)}) collective-permute-start(f32[4,8,128]{2,1,0:T(8,128)S(1)} %get-tuple-element.241), channel_id=1, source_target_pairs={{0,1},{1,2},{2,3},{3,4},{4,5},{5,6},{6,7},{8,9},{9,10},{10,11},{11... | collective-permute-start | bytes 49160 | tf_op jit(solution)/shard_map/ppermute | solution.py:15
  42.3 7.2 collective-permute-start.4
  46.8 6.8 collective-permute-start.3
  205.6 6.8 collective-permute-start.7
  215.0 6.8 collective-permute-start.9
  224.4 6.8 collective-permute-start.11
  233.7 6.8 collective-permute-start.13
  243.1 6.9 collective-permute-start.15
  252.5 6.8 collective-permute-start.17
  261.9 6.8 collective-permute-start.19
  295.1 7.3 collective-permute-start
  304.4 6.8 collective-permute-start.2
  312.3 7.3 collective-permute-start
  321.6 6.8 collective-permute-start.2
  329.5 7.3 collective-permute-start
  338.8 6.8 collective-permute-start.2
  346.7 7.3 collective-permute-start
  363.9 7.3 collective-permute-start
  373.2 6.8 collective-permute-start.2
  381.2 7.3 collective-permute-start
  390.5 6.8 collective-permute-start.2
  398.4 7.3 collective-permute-start
  407.7 6.8 collective-permute-start.2
  415.6 7.3 collective-permute-start
  424.9 6.8 collective-permute-start.2
  432.8 7.3 collective-permute-start
  442.1 6.8 collective-permute-start.2
  450.0 7.3 collective-permute-start
  459.3 6.8 collective-permute-start.2
  467.3 7.3 collective-permute-start
  476.5 6.8 collective-permute-start.2
  484.5 7.3 collective-permute-start
  493.8 6.8 collective-permute-start.2
  501.7 7.3 collective-permute-start
  511.0 6.8 collective-permute-start.2
  518.9 7.3 collective-permute-start
  528.2 6.8 collective-permute-start.2
  536.1 7.3 collective-permute-start
  545.4 6.8 collective-permute-start.2
  553.3 7.3 collective-permute-start
  562.6 6.8 collective-permute-start.2
  570.6 7.3 collective-permute-start
  579.8 6.8 collective-permute-start.2
  587.8 7.3 collective-permute-start
  597.1 6.8 collective-permute-start.2
  605.0 7.3 collective-permute-start
  622.2 7.3 collective-permute-start
  631.5 6.8 collective-permute-start.2
  639.4 7.3 collective-permute-start
  648.7 6.8 collective-permute-start.2
  656.7 7.3 collective-permute-start
  665.9 6.8 collective-permute-start.2
  673.9 7.3 collective-permute-start
  691.1 7.3 collective-permute-start
  708.3 7.3 collective-permute-start
  725.5 7.3 collective-permute-start
  742.7 7.3 collective-permute-start
  760.0 7.3 collective-permute-start
  777.2 7.3 collective-permute-start
  794.4 7.3 collective-permute-start
  811.6 7.3 collective-permute-start
  (69 other events, 444.4 us)
where the time goes:
time: 835 us; the launch traced here: 831 us
  starting transfers between devices  300 us (36%)
  waiting for transfers between devices  281 us (34%)
  other arithmetic  134 us (16%)
  local copies, waits for them, and re-layouts  111 us (13%)
    ppermute x31, waiting for transfers between devices, shifted(): return lax.ppermute(block, axis, route)  168 us
    ppermute x41, starting transfers between devices, padded_2(): lax.ppermute(lax.slice_in_dim(block, block.shape[dim] - width, None, axis...  158 us
    ppermute x41, waiting for transfers between devices, padded_2(): lax.ppermute(lax.slice_in_dim(block, block.shape[dim] - width, None, axis...  113 us
    ppermute x41, starting transfers between devices, padded_2(): lax.ppermute(lax.slice_in_dim(block, 0, width, axis=dim), axis, backward)  82.6 us
    reduce_sum x3, other arithmetic, restrict(): jnp.mean(reshaped, axis=(lead_rank + 1, lead_rank + 3, lead_rank + 5))  60.6 us
    ppermute x31, starting transfers between devices, shifted(): return lax.ppermute(block, axis, route)  59.5 us
    concatenate x1, local copies, waits for them, and re-layouts, padded_2(): block = jnp.concatenate([low, block, high], axis=dim)  32.1 us
    slice x1, local copies, waits for them, and re-layouts, advance(): speed = statics[direction]  28.4 us
  transfers between devices with their start and end apart: 113, of which 70 were waited for; matrix products, arithmetic and copies ran while one was open for 3% of the time, Pallas kernels for 0%

commit v1 on v0

v1 whole, which is shorter than its diff:
```python
import functools

import jax
import jax.numpy as jnp
from jax import lax
from jax.experimental import pallas as pl
from jax.experimental.pallas import tpu as pltpu
from jax.sharding import PartitionSpec as P

MESH = pl.DeviceIdType.MESH
W, HF, Z, Y = 16, 4, 16, 256
E = W + 2 * HF
CW, CZ, CY = W // 2, Z // 2, Y // 2
WIN = 5 * CW
TURNS = 4
F32 = jnp.float32


def up(x, axis):
    return pltpu.roll(x, x.shape[axis] - 1, axis)


def down(x, axis):
    return pltpu.roll(x, 1, axis)


def face(speed_a, speed_b, mix_a, mix_b, open_face, scale):
    f = 0.5 * (speed_a + speed_b) * open_face
    h = (0.5 * scale) * (mix_a + mix_b) * open_face
    return jnp.maximum(f, 0.0) + h, h - jnp.minimum(f, 0.0)


def make_coefs(stat, coef, lo, n, scale):
    u, w, v, k, m = stat
    ka, kb = k[lo - 1 : lo + n], k[lo : lo + n + 1]
    ma, mb = m[lo - 1 : lo + n], m[lo : lo + n + 1]
    a, b = face(u[lo - 1 : lo + n], u[lo : lo + n + 1], ka, kb, ma * mb, scale)
    own = slice(lo, lo + n)
    coef[1, own] = a[:n]
    coef[2, own] = b[1:]
    centre = 1.0 - (a[1:] + b[:n])
    kc, mc = kb[:n], mb[:n]
    for axis, field, low, high in ((1, w, 3, 4), (2, v, 5, 6)):
        c = field[own]
        extent = c.shape[axis]
        inside = lax.broadcasted_iota(jnp.int32, c.shape, axis) < extent - 1
        open_face = jnp.where(inside, mc * up(mc, axis), 0.0)
        a, b = face(c, up(c, axis), kc, up(kc, axis), open_face, scale)
        coef[low, own] = down(a, axis)
        coef[high, own] = b
        centre = centre - (a + down(b, axis))
    coef[0, own] = centre


def stencil(coef, q, lo, n):
    own = slice(lo, lo + n)
    c = q[own]
    x = coef[1, own] * q[lo - 1 : lo + n - 1] + coef[2, own] * q[lo + 1 : lo + n + 1]
    z = coef[3, own] * down(c, 1) + coef[4, own] * up(c, 1)
    y = coef[5, own] * down(c, 2) + coef[6, own] * up(c, 2)
    return (coef[0, own] * c + x) + (z + y)


def chunks(lo, hi, size):
    return [(i, min(size, hi - i)) for i in range(lo, hi, size)]


def pick(rows, cols, along):
    r = lax.broadcasted_iota(jnp.int32, (rows, cols), 0)
    c = lax.broadcasted_iota(jnp.int32, (rows, cols), 1)
    return jnp.where((r >> 1) == c if along == 0 else (c >> 1) == r, 1.0, 0.0).astype(F32)


def mul(a, b):
    return jnp.dot(a, b, precision=lax.Precision.HIGHEST, preferred_element_type=F32)


def restrict(pairs):
    flat = pairs.reshape(CW * Z, Y)
    narrow = mul(flat, pick(Y, CY, 0))
    short = mul(pick(CW * CZ, CW * Z, 1), narrow)
    return (0.125 * short).reshape(CW, CZ, CY)


def prolong(coarse):
    flat = mul(coarse.reshape(CW * CZ, CY), pick(CY, Y, 1))
    return mul(pick(CW * Z, CW * CZ, 0), flat).reshape(CW, Z, Y)


def kernel(
    T, S, D0,
    q_in, u_in, w_in, v_in, cls_in, msk_in, kd,
    out,
    st, ints, lv, coef, ends, pairs, s_own, s_next, r_own,
    cs_own, cs_win, ccoef, r_win, e_win, wb, d_out, d_in,
    loc_sem, h_send, h_recv, h2_send, h2_recv, s_sem, r_send, r_recv,
    c_send, c_recv, e_send, e_recv, d_send, d_recv, go,
):
    t, s = lax.axis_index("tm"), lax.axis_index("space")
    K = T // TURNS
    chain = t == D0

    def beside(step):
        return lax.rem(s + step + S, S)

    barrier = pltpu.get_barrier_semaphore()

    def greet(tm, space):
        pl.semaphore_signal(barrier, inc=1, device_id=(tm, space), device_id_type=MESH)

    for step in (-1, 1):
        pl.when((s + step >= 0) & (s + step < S))(functools.partial(greet, t, s + step))
    pl.when(t < T - 1)(lambda: greet(t + 1, s))
    pl.when(t != D0)(lambda: greet(D0, s))

    @pl.when(chain)
    def _():
        for step in (-2, 2):
            pl.when((s + step >= 0) & (s + step < S))(functools.partial(greet, t, s + step))

    fields = ((q_in, lv.at[0]), (u_in, st.at[0]), (w_in, st.at[1]), (v_in, st.at[2]),
              (cls_in, ints.at[0]), (msk_in, ints.at[1]))
    local = [pltpu.make_async_copy(src, dst.at[pl.ds(HF, W)], loc_sem.at[i])
             for i, (src, dst) in enumerate(fields)]
    for copy in local:
        copy.start()

    one = jnp.int32(1)
    zero = jnp.int32(0)

    def flag(condition):
        return jnp.where(condition, one, zero)

    expected = flag(s > 0) + flag(s < S - 1) + flag(t > 0)
    expected = expected + flag(chain) * (T - 1 + flag(s > 1) + flag(s < S - 2))
    pl.semaphore_wait(barrier, expected)

    def halo(i, side):
        src, dst = fields[i]
        src_lo, dst_lo = ((0, HF + W), (W - HF, 0))[side]
        return pltpu.make_async_remote_copy(
            src_ref=src.at[pl.ds(src_lo, HF)], dst_ref=dst.at[pl.ds(dst_lo, HF)],
            send_sem=h_send.at[i, side], recv_sem=h_recv.at[i, side],
            device_id=(t, beside(2 * side - 1)), device_id_type=MESH)

    def halo2(side):
        src_lo, dst_lo = ((HF, HF + W), (W, 0))[side]
        return pltpu.make_async_remote_copy(
            src_ref=lv.at[4, pl.ds(src_lo, HF)], dst_ref=lv.at[4, pl.ds(dst_lo, HF)],
            send_sem=h2_send.at[side], recv_sem=h2_recv.at[side],
            device_id=(t, beside(2 * side - 1)), device_id_type=MESH)

    has_target = (s > 0, s < S - 1)
    order = (1, 2, 3, 4, 5, 0)
    for i in order:
        for side in (0, 1):
            pl.when(has_target[side])(lambda i=i, side=side: halo(i, side).start())

    for has, lo in ((s > 0, 0), (s < S - 1, HF + W)):
        @pl.when(jnp.logical_not(has))
        def _(lo=lo):
            edge = slice(lo, lo + HF)
            blank = jnp.zeros((HF, Z, Y), F32)
            for i in range(3):
                st[i, edge] = blank
            for i in range(2):
                ints[i, edge] = jnp.zeros((HF, Z, Y), jnp.int32)
            lv[0, edge] = blank
            lv[4, edge] = blank

    @pl.when(chain)
    def _():
        def tell(n, carry):
            @pl.when(n != D0)
            def _():
                pl.semaphore_signal(go, inc=1, device_id=(n, s), device_id_type=MESH)
            return carry
        lax.fori_loop(0, T, tell, 0)
        for has, lo in ((s > 1, 0), (s > 0, CW), (s < S - 1, 3 * CW), (s < S - 2, 4 * CW)):
            @pl.when(jnp.logical_not(has))
            def _(lo=lo):
                blank = jnp.zeros((CW, CZ, CY), F32)
                for i in range(5):
                    cs_win[i, lo : lo + CW] = blank

                def clear(n, carry):
                    r_win[n, lo : lo + CW] = blank
                    return carry
                lax.fori_loop(0, T, clear, 0)

                def clear_e(n, carry):
                    e_win[n, lo : lo + CW] = blank
                    return carry
                lax.fori_loop(0, K, clear_e, 0)

    for copy in local:
        copy.wait()

    def widen(lo, n):
        own = slice(lo, lo + n)
        cls = ints[0, own]
        kappa = jnp.zeros(cls.shape, F32)
        for i in range(8):
            kappa = jnp.where(cls == i, kd[i], kappa)
        st[3, own] = kappa
        st[4, own] = ints[1, own].astype(F32)

    def sum_pairs(src, lo):
        for i in range(CW):
            pairs[i] = src[lo + 2 * i] + src[lo + 2 * i + 1]

    sum_pairs(lv.at[0], HF)
    s_own[...] = restrict(pairs[...])
    start_copy = pltpu.make_async_remote_copy(
        src_ref=s_own, dst_ref=s_next, send_sem=s_sem.at[0], recv_sem=s_sem.at[1],
        device_id=(lax.rem(t + T - 1, T), s), device_id_type=MESH)
    pl.when(t > 0)(lambda: start_copy.start())

    stat = [st.at[i] for i in range(5)]
    for lo, n in chunks(HF, HF + W, 2):
        widen(lo, n)
    for lo, n in chunks(HF + 1, HF + W - 1, 2):
        make_coefs(stat, coef, lo, n, 1.0)

    def to_slab(src, dst_of, send, recv, step):
        return pltpu.make_async_remote_copy(
            src_ref=src, dst_ref=dst_of((2 - step) * CW), send_sem=send, recv_sem=recv,
            device_id=(t, beside(step)), device_id_type=MESH)

    steps = (-2, 2, -1, 1)

    def there(step):
        return (s + step >= 0) & (s + step < S)

    def cs_copy(j):
        return to_slab(cs_own, lambda lo: cs_win.at[:, pl.ds(lo, CW)],
                       c_send.at[j], c_recv.at[j], steps[j])

    @pl.when(chain)
    def _():
        for i in range(5):
            sum_pairs(st.at[i], HF)
            part = restrict(pairs[...])
            cs_own[i] = part
            cs_win[i, 2 * CW : 3 * CW] = part
        for j in range(4):
            pl.when(there(steps[j]))(lambda j=j: cs_copy(j).start())

    def fine(src, dst, shift, lo, hi):
        for i, n in chunks(lo, hi, 2):
            dst[i - shift : i - shift + n] = stencil(coef, src, i, n)

    def inner(base):
        for j in range(1, HF + 1):
            last = base + j == 2 * HF
            dst, shift = (ends, HF) if last else (lv.at[base + j], 0)
            fine(lv.at[base + j - 1], dst, shift, HF + j, HF + W - j)

    def outer(base):
        for j in range(1, HF + 1):
            last = base + j == 2 * HF
            dst, shift = (ends, HF) if last else (lv.at[base + j], 0)
            fine(lv.at[base + j - 1], dst, shift, j, HF + j)
            fine(lv.at[base + j - 1], dst, shift, HF + W - j, E - j)

    inner(0)
    for i in order:
        for side in (0, 1):
            pl.when(has_target[1 - side])(lambda i=i, side=side: halo(i, side).wait_recv())
    for lo in (0, HF + W):
        for i, n in chunks(lo, lo + HF, 2):
            widen(i, n)
    for lo in (1, HF + W - 1):
        for i, n in chunks(lo, lo + HF, 2):
            make_coefs(stat, coef, i, n, 1.0)
    outer(0)
    for side in (0, 1):
        pl.when(has_target[side])(lambda side=side: halo2(side).start())
    inner(HF)
    for side in (0, 1):
        pl.when(has_target[1 - side])(lambda side=side: halo2(side).wait_recv())
    outer(HF)

    sum_pairs(ends, 0)
    pl.when(t < T - 1)(lambda: start_copy.wait_recv())
    pl.when(t != D0)(lambda: pl.semaphore_wait(go, 1))

    def r_copy(n, kind, j):
        step = (0,) + steps
        step = step[j]
        size = CW if step == 0 or (abs(step) == 1 and kind < 2) else CW // 2
        lo = CW - size if step > 0 else 0
        return pltpu.make_async_remote_copy(
            src_ref=r_own.at[pl.ds(lo, size)],
            dst_ref=r_win.at[n, pl.ds((2 - step) * CW + lo, size)],
            send_sem=r_send.at[j], recv_sem=r_recv.at[n, j],
            device_id=(D0, beside(step)), device_id_type=MESH)

    pieces = ((0, 1, 2, 3, 4), (0, 3, 4), (0, 3, 4), (0,))

    def r_each(n, act, wait):
        for kind in range(TURNS):
            @pl.when(lax.rem(n, TURNS) == kind)
            def _(kind=kind):
                r_pieces(n, kind, act, wait)

    def r_pieces(n, kind, act, wait):
        for j in pieces[kind]:
            step = ((0,) + steps)[j]
            condition = (n != D0) if step == 0 else there(-step if wait else step)
            pl.when(condition)(lambda j=j: act(r_copy(n, kind, j)))

    @pl.when(t < T - 1)
    def _():
        r_own[...] = restrict(pairs[...]) - s_next[...]

        @pl.when(chain)
        def _():
            r_win[D0, 2 * CW : 3 * CW] = r_own[...]
        r_each(t, lambda copy: copy.start(), False)

    def d_copy(n):
        return pltpu.make_async_remote_copy(
            src_ref=d_out.at[n], dst_ref=d_in, send_sem=d_send.at[n], recv_sem=d_recv,
            device_id=(n, s), device_id_type=MESH)

    def e_copy(k, j):
        return to_slab(e_win.at[k, pl.ds(2 * CW, CW)], lambda lo: e_win.at[k, pl.ds(lo, CW)],
                       e_send.at[k, j], e_recv.at[k, j], steps[j])

    def turn(n, kind, src, dst, last):
        lo, hi = 4 * kind, WIN - 4 * kind
        for j in range(1, 4):
            for i, m in chunks(lo + j, hi - j, CW):
                wb[1 - j % 2, i : i + m] = stencil(ccoef, src, i, m)
            src = wb.at[1 - j % 2]
        if not last:
            r_pieces(n, kind, lambda copy: copy.wait_recv(), True)
        own_lo, own_hi = 2 * CW, 3 * CW
        parts = chunks(lo + 4, own_lo, CW) + [(own_lo, CW)] + chunks(own_hi, hi - 4, CW)
        for i, m in parts:
            fresh = stencil(ccoef, src, i, m)
            if i != own_lo:
                dst[i : i + m] = fresh + r_win[n, i : i + m]
                continue
            d_out[n] = fresh
            if not last:
                dst[i : i + m] = fresh + r_win[n, i : i + m]

        @pl.when(n != D0)
        def _():
            d_copy(n).start()

        @pl.when(n == D0)
        def _():
            d_in[...] = d_out[n]

    @pl.when(chain)
    def _():
        for j in range(4):
            pl.when(there(-steps[j]))(lambda j=j: cs_copy(j).wait_recv())
        cstat = [cs_win.at[i] for i in range(5)]
        for lo, n in chunks(1, WIN - 1, 4):
            make_coefs(cstat, ccoef, lo, n, 0.5)

        r_pieces(0, 0, lambda copy: copy.wait_recv(), True)
        src = r_win.at[0]
        for kind in range(1, TURNS):
            dst = wb.at[1] if kind < TURNS - 1 else e_win.at[1]
            turn(kind, kind, src, dst, False)
            src = wb.at[1]

        def cycle(k, final):
            for j in range(4):
                pl.when(there(steps[j]))(lambda j=j: e_copy(k, j).start())
            for j in range(4):
                pl.when(there(-steps[j]))(lambda j=j: e_copy(k, j).wait_recv())
            src = e_win.at[k]
            for kind in range(TURNS):
                last = kind == TURNS - 1
                dst = (None if final else e_win.at[k + 1]) if last else wb.at[1]
                turn(TURNS * k + kind, kind, src, dst, final and last)
                src = wb.at[1]

        def body(k, carry):
            cycle(k, False)
            return carry
        lax.fori_loop(1, K - 1, body, 0)
        cycle(K - 1, True)

    pl.when((t > 0) & (t != D0))(lambda: d_copy(t).wait_recv())

    @pl.when(t == 0)
    def _():
        out[...] = ends[...]

    @pl.when(t > 0)
    def _():
        fine_delta = prolong(d_in[...])
        for i in range(CW):
            out[2 * i] = ends[2 * i] + fine_delta[i]
            out[2 * i + 1] = ends[2 * i + 1] + fine_delta[i]

    for side in (0, 1):
        for i in order:
            pl.when(has_target[side])(lambda i=i, side=side: halo(i, side).wait_send())
        pl.when(has_target[side])(lambda side=side: halo2(side).wait_send())
    pl.when(t > 0)(lambda: start_copy.wait_send())
    pl.when(t < T - 1)(lambda: r_each(t, lambda copy: copy.wait_send(), False))

    @pl.when(chain)
    def _():
        for j in range(4):
            pl.when(there(steps[j]))(lambda j=j: cs_copy(j).wait_send())

        def drain_e(k, carry):
            for j in range(4):
                pl.when(there(steps[j]))(lambda j=j: e_copy(k, j).wait_send())
            return carry
        lax.fori_loop(1, K, drain_e, 0)

        def drain_d(n, carry):
            pl.when(n != D0)(lambda: d_copy(n).wait_send())
            return carry
        lax.fori_loop(1, T, drain_d, 0)


def shards(starts, u, w, v, cls, msk, kd):
    T, S = lax.axis_size("tm"), lax.axis_size("space")
    K = T // TURNS
    D0 = (3 * T) // 4
    dma = pltpu.SemaphoreType.DMA
    anywhere = pl.BlockSpec(memory_space=pl.ANY)
    slab = (CW, CZ, CY)
    result = pl.pallas_call(
        functools.partial(kernel, T, S, D0),
        out_shape=jax.ShapeDtypeStruct((W, Z, Y), F32),
        in_specs=[anywhere] * 6 + [pl.BlockSpec(memory_space=pltpu.SMEM)],
        out_specs=pl.BlockSpec(memory_space=pltpu.VMEM),
        scratch_shapes=[
            pltpu.VMEM((5, E, Z, Y), F32),
            pltpu.VMEM((2, E, Z, Y), jnp.int32),
            pltpu.VMEM((8, E, Z, Y), F32),
            pltpu.VMEM((7, E, Z, Y), F32),
            pltpu.VMEM((W, Z, Y), F32),
            pltpu.VMEM((CW, Z, Y), F32),
            pltpu.VMEM(slab, F32),
            pltpu.VMEM(slab, F32),
            pltpu.VMEM(slab, F32),
            pltpu.VMEM((5,) + slab, F32),
            pltpu.VMEM((5, WIN, CZ, CY), F32),
            pltpu.VMEM((7, WIN, CZ, CY), F32),
            pltpu.VMEM((T, WIN, CZ, CY), F32),
            pltpu.VMEM((K, WIN, CZ, CY), F32),
            pltpu.VMEM((2, WIN, CZ, CY), F32),
            pltpu.VMEM((T,) + slab, F32),
            pltpu.VMEM(slab, F32),
            dma((6,)),
            dma((6, 2)), dma((6, 2)),
            dma((2,)), dma((2,)),
            dma((2,)),
            dma((5,)), dma((T, 5)),
            dma((4,)), dma((4,)),
            dma((K, 4)), dma((K, 4)),
            dma((T,)), dma(()),
            pltpu.SemaphoreType.REGULAR,
        ],
        compiler_params=pltpu.CompilerParams(
            collective_id=0, has_side_effects=True, vmem_limit_bytes=56 * 1024 * 1024),
    )(starts[0], u, w, v, cls, msk, kd)
    return result[None]


def solution(mesh):
    slabs = P("space", None, None)
    return jax.shard_map(
        shards, mesh=mesh,
        in_specs=(P("tm", "space", None, None),) + (slabs,) * 5 + (P(),),
        out_specs=P("tm", "space", None, None), check_vma=False)
```

time: 835 us -> 80.6 us (0.10)
  the two profiles are of different devices: /device:TPU:130 before, /device:TPU:23 now
where the time goes in v1:
time: 80.6 us; the launch traced here: 79.8 us
  Pallas kernels  78.1 us (97%)
  local copies, waits for them, and re-layouts  1.67 us (2%)
    pallas_call x1, Pallas kernels, shards(): pl.pallas_call(functools.partial(kernel, T, S, D0), out_shape=jax.ShapeDt...  78.1 us
    unnamed x1, local copies, waits for them, and re-layouts  1.67 us

profile of v1, /device:TPU:23, one launch (start us, length us, event | category | flops | bytes accessed | tf_op | source)
XLA Modules:
  0.0 79.8 jit_solution(5737968059313975923)
XLA Ops:
  0.0 78.1 %shard_map.73 = f32[16,16,256]{2,1,0:T(8,128)} custom-call(f32[16,16,256]{2,1,0:T(8,128)} %bitcast.3, f32[16,16,256]{2,1,0:T(8,128)} %u_in.1, f32[16,16,256]{2,1,0:T(8,128)} %w_in.1, f32[16,16,256]{2,1,0:T(8,128)} %v_in.1, s32[16,16,256]{2,1,0:T(8,128)} %cls_in.1, s32[16,16,256]{2,1,0:T(8,128)} %msk_in.1, f32[8]{0:T(128)} %kd.1), custom_call_target="tpu_custom_call" | custom-call | tf_op jit(solution)/shard_map/pallas_call | solution.py:435
  78.1 1.7 %copy.9 = f32[1,16,16,256]{3,2,1,0:T(8,128)} copy(f32[1,16,16,256]{3,2,1,0:T(8,128)} %bitcast.2) | data formatting | bytes 524288

commit v2 on v1

--- a/solution.py
+++ b/solution.py
@@ -13,6 +13,7 @@
 CW, CZ, CY = W // 2, Z // 2, Y // 2
 WIN = 5 * CW
 TURNS = 4
+GROUP = 2 * TURNS
 F32 = jnp.float32
 
 
@@ -88,17 +89,23 @@
 
 
 def kernel(
-    T, S, D0,
+    T, S,
     q_in, u_in, w_in, v_in, cls_in, msk_in, kd,
     out,
     st, ints, lv, coef, ends, pairs, s_own, s_next, r_own,
     cs_own, cs_win, ccoef, r_win, e_win, wb, d_out, d_in,
+    cs_full, fcoef, p_own, p_full, cur, g_out, g_in,
     loc_sem, h_send, h_recv, h2_send, h2_recv, s_sem, r_send, r_recv,
-    c_send, c_recv, e_send, e_recv, d_send, d_recv, go,
+    c_send, c_recv, e_send, e_recv, d_send, d_recv,
+    f_send, f_recv, p_send, p_recv, g_send, g_recv, go,
 ):
     t, s = lax.axis_index("tm"), lax.axis_index("space")
-    K = T // TURNS
-    chain = t == D0
+    groups = T // GROUP
+    MAIN = T - GROUP
+    slot = lax.rem(t, GROUP)
+    home = t - slot
+    chain = slot == 0
+    main = t == MAIN
 
     def beside(step):
         return lax.rem(s + step + S, S)
@@ -111,12 +118,20 @@
     for step in (-1, 1):
         pl.when((s + step >= 0) & (s + step < S))(functools.partial(greet, t, s + step))
     pl.when(t < T - 1)(lambda: greet(t + 1, s))
-    pl.when(t != D0)(lambda: greet(D0, s))
+    pl.when(slot != 0)(lambda: greet(home, s))
+    pl.when((t >= GROUP) & (t != MAIN))(lambda: greet(MAIN, s))
 
     @pl.when(chain)
     def _():
         for step in (-2, 2):
             pl.when((s + step >= 0) & (s + step < S))(functools.partial(greet, t, s + step))
+
+    @pl.when(main)
+    def _():
+        for z in range(S):
+            for x in range(groups - 1):
+                greet(x * GROUP, z)
+            pl.when(s != z)(functools.partial(greet, t, z))
 
     fields = ((q_in, lv.at[0]), (u_in, st.at[0]), (w_in, st.at[1]), (v_in, st.at[2]),
               (cls_in, ints.at[0]), (msk_in, ints.at[1]))
@@ -132,7 +147,8 @@
         return jnp.where(condition, one, zero)
 
     expected = flag(s > 0) + flag(s < S - 1) + flag(t > 0)
-    expected = expected + flag(chain) * (T - 1 + flag(s > 1) + flag(s < S - 2))
+    expected = expected + flag(chain) * (GROUP - 1 + flag(s > 1) + flag(s < S - 2))
+    expected = expected + flag(chain & (t != MAIN)) * S + flag(main) * (T - GROUP - 1 + S - 1)
     pl.semaphore_wait(barrier, expected)
 
     def halo(i, side):
@@ -170,12 +186,8 @@
 
     @pl.when(chain)
     def _():
-        def tell(n, carry):
-            @pl.when(n != D0)
-            def _():
-                pl.semaphore_signal(go, inc=1, device_id=(n, s), device_id_type=MESH)
-            return carry
-        lax.fori_loop(0, T, tell, 0)
+        for n in range(1, GROUP):
+            pl.semaphore_signal(go, inc=1, device_id=(home + n, s), device_id_type=MESH)
         for has, lo in ((s > 1, 0), (s > 0, CW), (s < S - 1, 3 * CW), (s < S - 2, 4 * CW)):
             @pl.when(jnp.logical_not(has))
             def _(lo=lo):
@@ -183,15 +195,20 @@
                 for i in range(5):
                     cs_win[i, lo : lo + CW] = blank
 
-                def clear(n, carry):
+                for n in range(GROUP):
                     r_win[n, lo : lo + CW] = blank
-                    return carry
-                lax.fori_loop(0, T, clear, 0)
-
-                def clear_e(n, carry):
-                    e_win[n, lo : lo + CW] = blank
-                    return carry
-                lax.fori_loop(0, K, clear_e, 0)
+                e_win[lo : lo + CW] = blank
+
+    @pl.when(main)
+    def _():
+        margin = jnp.zeros((1, CZ, CY), F32)
+        for lo in (0, S * CW + 1):
+            for i in range(5):
+                cs_full[i, lo : lo + 1] = margin
+            for i in range(3):
+                cur[i, lo : lo + 1] = margin
+        for i in range(S):
+            cur[0, 1 + i * CW : 1 + (i + 1) * CW] = jnp.zeros((CW, CZ, CY), F32)
 
     for copy in local:
         copy.wait()
@@ -245,6 +262,22 @@
             cs_win[i, 2 * CW : 3 * CW] = part
         for j in range(4):
             pl.when(there(steps[j]))(lambda j=j: cs_copy(j).start())
+
+    def f_copy(z):
+        return pltpu.make_async_remote_copy(
+            src_ref=cs_own, dst_ref=cs_full.at[:, pl.ds(1 + s * CW, CW)],
+            send_sem=f_send.at[z], recv_sem=f_recv.at[s],
+            device_id=(MAIN, z), device_id_type=MESH)
+
+    def f_arrival(z):
+        return pltpu.make_async_remote_copy(
+            src_ref=cs_own, dst_ref=cs_full.at[:, pl.ds(1 + z * CW, CW)],
+            send_sem=f_send.at[z], recv_sem=f_recv.at[z],
+            device_id=(MAIN, z), device_id_type=MESH)
+
+    @pl.when(main)
+    def _():
+        cs_full[:, pl.ds(1 + s * CW, CW)] = cs_own[...]
 
     def fine(src, dst, shift, lo, hi):
         for i, n in chunks(lo, hi, 2):
@@ -276,6 +309,12 @@
     outer(0)
     for side in (0, 1):
         pl.when(has_target[side])(lambda side=side: halo2(side).start())
+
+    @pl.when(main)
+    def _():
+        for z in range(S):
+            pl.when(s != z)(lambda z=z: f_copy(z).start())
+
     inner(HF)
     for side in (0, 1):
         pl.when(has_target[1 - side])(lambda side=side: halo2(side).wait_recv())
@@ -283,7 +322,7 @@
 
     sum_pairs(ends, 0)
     pl.when(t < T - 1)(lambda: start_copy.wait_recv())
-    pl.when(t != D0)(lambda: pl.semaphore_wait(go, 1))
+    pl.when(slot != 0)(lambda: pl.semaphore_wait(go, 1))
 
     def r_copy(n, kind, j):
         step = (0,) + steps
@@ -294,7 +333,7 @@
             src_ref=r_own.at[pl.ds(lo, size)],
             dst_ref=r_win.at[n, pl.ds((2 - step) * CW + lo, size)],
             send_sem=r_send.at[j], recv_sem=r_recv.at[n, j],
-            device_id=(D0, beside(step)), device_id_type=MESH)
+            device_id=(home, beside(step)), device_id_type=MESH)
 
     pieces = ((0, 1, 2, 3, 4), (0, 3, 4), (0, 3, 4), (0,))
 
@@ -307,8 +346,12 @@
     def r_pieces(n, kind, act, wait):
         for j in pieces[kind]:
             step = ((0,) + steps)[j]
-            condition = (n != D0) if step == 0 else there(-step if wait else step)
-            pl.when(condition)(lambda j=j: act(r_copy(n, kind, j)))
+            own_slab = n != 0
+            condition = own_slab if step == 0 else there(-step if wait else step)
+            if condition is True:
+                act(r_copy(n, kind, j))
+            elif condition is not False:
+                pl.when(condition)(lambda j=j: act(r_copy(n, kind, j)))
 
     @pl.when(t < T - 1)
     def _():
@@ -316,44 +359,54 @@
 
         @pl.when(chain)
         def _():
-            r_win[D0, 2 * CW : 3 * CW] = r_own[...]
-        r_each(t, lambda copy: copy.start(), False)
+            r_win[0, 2 * CW : 3 * CW] = r_own[...]
+        r_each(slot, lambda copy: copy.start(), False)
 
     def d_copy(n):
         return pltpu.make_async_remote_copy(
             src_ref=d_out.at[n], dst_ref=d_in, send_sem=d_send.at[n], recv_sem=d_recv,
-            device_id=(n, s), device_id_type=MESH)
-
-    def e_copy(k, j):
-        return to_slab(e_win.at[k, pl.ds(2 * CW, CW)], lambda lo: e_win.at[k, pl.ds(lo, CW)],
-                       e_send.at[k, j], e_recv.at[k, j], steps[j])
-
-    def turn(n, kind, src, dst, last):
+            device_id=(home + n, s), device_id_type=MESH)
+
+    def e_copy(j):
+        return to_slab(e_win.at[pl.ds(2 * CW, CW)], lambda lo: e_win.at[pl.ds(lo, CW)],
+                       e_send.at[j], e_recv.at[j], steps[j])
+
+    def p_copy(z):
+        return pltpu.make_async_remote_copy(
+            src_ref=p_own, dst_ref=p_full.at[home // GROUP, pl.ds(s * CW, CW)],
+            send_sem=p_send.at[z], recv_sem=p_recv.at[home // GROUP, s],
+            device_id=(MAIN, z), device_id_type=MESH)
+
+    def p_arrival(x, z):
+        return pltpu.make_async_remote_copy(
+            src_ref=p_own, dst_ref=p_full.at[x, pl.ds(z * CW, CW)],
+            send_sem=p_send.at[z], recv_sem=p_recv.at[x, z],
+            device_id=(MAIN, z), device_id_type=MESH)
+
+    def turn(n, src, dst):
+        kind = n % TURNS
         lo, hi = 4 * kind, WIN - 4 * kind
         for j in range(1, 4):
             for i, m in chunks(lo + j, hi - j, CW):
                 wb[1 - j % 2, i : i + m] = stencil(ccoef, src, i, m)
             src = wb.at[1 - j % 2]
-        if not last:
-            r_pieces(n, kind, lambda copy: copy.wait_recv(), True)
         own_lo, own_hi = 2 * CW, 3 * CW
-        parts = chunks(lo + 4, own_lo, CW) + [(own_lo, CW)] + chunks(own_hi, hi - 4, CW)
-        for i, m in parts:
-            fresh = stencil(ccoef, src, i, m)
-            if i != own_lo:
-                dst[i : i + m] = fresh + r_win[n, i : i + m]
-                continue
-            d_out[n] = fresh
-            if not last:
-                dst[i : i + m] = fresh + r_win[n, i : i + m]
-
-        @pl.when(n != D0)
-        def _():
-            d_copy(n).start()
-
-        @pl.when(n == D0)
-        def _():
-            d_in[...] = d_out[n]
+        d_out[n] = stencil(ccoef, src, own_lo, CW)
+        d_copy(n).start()
+
+        if n == GROUP - 1:
+            @pl.when(t != MAIN)
+            def _():
+                r_pieces(n, kind, lambda copy: copy.wait_recv(), True)
+                p_own[...] = d_out[n] + r_win[n, own_lo:own_hi]
+                for z in range(S):
+                    p_copy(z).start()
+            return
+        r_pieces(n, kind, lambda copy: copy.wait_recv(), True)
+        into = slice(own_lo, own_hi)
+        dst[into] = d_out[n] + r_win[n, into]
+        for i, m in chunks(lo + 4, own_lo, CW) + chunks(own_hi, hi - 4, CW):
+            dst[i : i + m] = stencil(ccoef, src, i, m) + r_win[n, i : i + m]
 
     @pl.when(chain)
     def _():
@@ -365,75 +418,108 @@
 
         r_pieces(0, 0, lambda copy: copy.wait_recv(), True)
         src = r_win.at[0]
-        for kind in range(1, TURNS):
-            dst = wb.at[1] if kind < TURNS - 1 else e_win.at[1]
-            turn(kind, kind, src, dst, False)
+        for n in range(1, TURNS):
+            turn(n, src, wb.at[1] if n < TURNS - 1 else e_win)
             src = wb.at[1]
-
-        def cycle(k, final):
-            for j in range(4):
-                pl.when(there(steps[j]))(lambda j=j: e_copy(k, j).start())
-            for j in range(4):
-                pl.when(there(-steps[j]))(lambda j=j: e_copy(k, j).wait_recv())
-            src = e_win.at[k]
-            for kind in range(TURNS):
-                last = kind == TURNS - 1
-                dst = (None if final else e_win.at[k + 1]) if last else wb.at[1]
-                turn(TURNS * k + kind, kind, src, dst, final and last)
-                src = wb.at[1]
-
-        def body(k, carry):
-            cycle(k, False)
+        for j in range(4):
+            pl.when(there(steps[j]))(lambda j=j: e_copy(j).start())
+        for j in range(4):
+            pl.when(there(-steps[j]))(lambda j=j: e_copy(j).wait_recv())
+        src = e_win
+        for n in range(TURNS, GROUP):
+            turn(n, src, wb.at[1])
+            src = wb.at[1]
+
+    def g_copy(m):
+        return pltpu.make_async_remote_copy(
+            src_ref=g_out.at[m], dst_ref=g_in, send_sem=g_send.at[m], recv_sem=g_recv,
+            device_id=(m + GROUP, s), device_id_type=MESH)
+
+    @pl.when(main)
+    def _():
+        for z in range(S):
+            pl.when(s != z)(lambda z=z: f_arrival(z).wait_recv())
+        fstat = [cs_full.at[i] for i in range(5)]
+        for lo, n in chunks(1, S * CW + 1, 4):
+            make_coefs(fstat, fcoef, lo, n, 0.5)
+
+        def big_turn(m, carry):
+            @pl.when(lax.rem(m, GROUP) == 0)
+            def _():
+                x = m // GROUP
+                for z in range(S):
+                    p_arrival(x, z).wait_recv()
+                for i, n in chunks(0, S * CW, CW):
+                    cur[0, i + 1 : i + 1 + n] = cur[0, i + 1 : i + 1 + n] + p_full[x, i : i + n]
+
+            for a, b in ((0, 1), (1, 2), (2, 1), (1, 0)):
+                for i, n in chunks(1, S * CW + 1, CW):
+                    cur[b, i : i + n] = stencil(fcoef, cur.at[a], i, n)
+            g_out[m] = cur[0, pl.ds(1 + s * CW, CW)]
+            pl.when(m + GROUP != MAIN)(lambda: g_copy(m).start())
             return carry
-        lax.fori_loop(1, K - 1, body, 0)
-        cycle(K - 1, True)
-
-    pl.when((t > 0) & (t != D0))(lambda: d_copy(t).wait_recv())
-
-    @pl.when(t == 0)
-    def _():
-        out[...] = ends[...]
-
-    @pl.when(t > 0)
-    def _():
-        fine_delta = prolong(d_in[...])
-        for i in range(CW):
-            out[2 * i] = ends[2 * i] + fine_delta[i]
-            out[2 * i + 1] = ends[2 * i + 1] + fine_delta[i]
+        lax.fori_loop(0, T - GROUP, big_turn, 0)
+
+    pl.when(slot > 0)(lambda: d_copy(slot).wait_recv())
+    pl.when((t >= GROUP) & (t != MAIN))(lambda: g_copy(t - GROUP).wait_recv())
+
+    @pl.when(main)
+    def _():
+        g_in[...] = g_out[MAIN - GROUP]
+
+    @pl.when(slot == 0)
+    def _():
+        d_in[...] = jnp.zeros((CW, CZ, CY), F32)
+
+    @pl.when(t >= GROUP)
+    def _():
+        d_in[...] = d_in[...] + g_in[...]
+
+    fine_delta = prolong(d_in[...])
+    for i in range(CW):
+        out[2 * i] = ends[2 * i] + fine_delta[i]
+        out[2 * i + 1] = ends[2 * i + 1] + fine_delta[i]
 
     for side in (0, 1):
         for i in order:
             pl.when(has_target[side])(lambda i=i, side=side: halo(i, side).wait_send())
         pl.when(has_target[side])(lambda side=side: halo2(side).wait_send())
     pl.when(t > 0)(lambda: start_copy.wait_send())
-    pl.when(t < T - 1)(lambda: r_each(t, lambda copy: copy.wait_send(), False))
+    pl.when(t < T - 1)(lambda: r_each(slot, lambda copy: copy.wait_send(), False))
 
     @pl.when(chain)
     def _():
         for j in range(4):
             pl.when(there(steps[j]))(lambda j=j: cs_copy(j).wait_send())
 
-        def drain_e(k, carry):
-            for j in range(4):
-                pl.when(there(steps[j]))(lambda j=j: e_copy(k, j).wait_send())
+            pl.when(there(steps[j]))(lambda j=j: e_copy(j).wait_send())
+        for n in range(1, GROUP):
+            d_copy(n).wait_send()
+
+        @pl.when(t != MAIN)
+        def _():
+            for z in range(S):
+                p_copy(z).wait_send()
+
+    @pl.when(main)
+    def _():
+        for z in range(S):
+            pl.when(s != z)(lambda z=z: f_copy(z).wait_send())
+
+        def drain(m, carry):
+            pl.when(m + GROUP != MAIN)(lambda: g_copy(m).wait_send())
             return carry
-        lax.fori_loop(1, K, drain_e, 0)
-
-        def drain_d(n, carry):
-            pl.when(n != D0)(lambda: d_copy(n).wait_send())
-            return carry
-        lax.fori_loop(1, T, drain_d, 0)
+        lax.fori_loop(0, T - GROUP, drain, 0)
 
 
 def shards(starts, u, w, v, cls, msk, kd):
     T, S = lax.axis_size("tm"), lax.axis_size("space")
-    K = T // TURNS
-    D0 = (3 * T) // 4
+    groups = T // GROUP
     dma = pltpu.SemaphoreType.DMA
     anywhere = pl.BlockSpec(memory_space=pl.ANY)
     slab = (CW, CZ, CY)
     result = pl.pallas_call(
-        functools.partial(kernel, T, S, D0),
+        functools.partial(kernel, T, S),
         out_shape=jax.ShapeDtypeStruct((W, Z, Y), F32),
         in_specs=[anywhere] * 6 + [pl.BlockSpec(memory_space=pltpu.SMEM)],
         out_specs=pl.BlockSpec(memory_space=pltpu.VMEM),
@@ -450,19 +536,29 @@
             pltpu.VMEM((5,) + slab, F32),
             pltpu.VMEM((5, WIN, CZ, CY), F32),
             pltpu.VMEM((7, WIN, CZ, CY), F32),
-            pltpu.VMEM((T, WIN, CZ, CY), F32),
-            pltpu.VMEM((K, WIN, CZ, CY), F32),
+            pltpu.VMEM((GROUP, WIN, CZ, CY), F32),
+            pltpu.VMEM((WIN, CZ, CY), F32),
             pltpu.VMEM((2, WIN, CZ, CY), F32),
-            pltpu.VMEM((T,) + slab, F32),
+            pltpu.VMEM((GROUP,) + slab, F32),
+            pltpu.VMEM(slab, F32),
+            pltpu.VMEM((5, S * CW + 2, CZ, CY), F32),
+            pltpu.VMEM((7, S * CW + 2, CZ, CY), F32),
+            pltpu.VMEM(slab, F32),
+            pltpu.VMEM((groups - 1, S * CW, CZ, CY), F32),
+            pltpu.VMEM((3, S * CW + 2, CZ, CY), F32),
+            pltpu.VMEM((T - GROUP,) + slab, F32),
             pltpu.VMEM(slab, F32),
             dma((6,)),
             dma((6, 2)), dma((6, 2)),
             dma((2,)), dma((2,)),
             dma((2,)),
-            dma((5,)), dma((T, 5)),
+            dma((5,)), dma((GROUP, 5)),
             dma((4,)), dma((4,)),
-            dma((K, 4)), dma((K, 4)),
-            dma((T,)), dma(()),
+            dma((4,)), dma((4,)),
+            dma((GROUP,)), dma(()),
+            dma((S,)), dma((S,)),
+            dma((S,)), dma((groups - 1, S)),
+            dma((T - GROUP,)), dma(()),
             pltpu.SemaphoreType.REGULAR,
         ],
         compiler_params=pltpu.CompilerParams(

time: 80.6 us -> 67.8 us (0.84)
  Pallas kernels: 78.1 us -> 64.9 us
    pallas_call x1, Pallas kernels: 78.1 us -> 64.9 us  [shards(): pl.pallas_call(functools.partial(kernel, T, S), out_shape=jax.ShapeDtypeS...]
where the time goes in v2:
time: 67.8 us; the launch traced here: 66.5 us
  Pallas kernels  64.9 us (96%)
  local copies, waits for them, and re-layouts  1.67 us (2%)
    pallas_call x1, Pallas kernels, shards(): pl.pallas_call(functools.partial(kernel, T, S), out_shape=jax.ShapeDtypeS...  64.9 us
    unnamed x1, local copies, waits for them, and re-layouts  1.67 us

profile of v2, /device:TPU:23, one launch (start us, length us, event | category | flops | bytes accessed | tf_op | source)
XLA Modules:
  0.0 66.5 jit_solution(9599258534679820492)
XLA Ops:
  0.0 64.9 %shard_map.73 = f32[16,16,256]{2,1,0:T(8,128)} custom-call(f32[16,16,256]{2,1,0:T(8,128)} %bitcast.3, f32[16,16,256]{2,1,0:T(8,128)} %u_in.1, f32[16,16,256]{2,1,0:T(8,128)} %w_in.1, f32[16,16,256]{2,1,0:T(8,128)} %v_in.1, s32[16,16,256]{2,1,0:T(8,128)} %cls_in.1, s32[16,16,256]{2,1,0:T(8,128)} %msk_in.1, f32[8]{0:T(128)} %kd.1), custom_call_target="tpu_custom_call" | custom-call | tf_op jit(solution)/shard_map/pallas_call | solution.py:521
  64.9 1.7 %copy.9 = f32[1,16,16,256]{3,2,1,0:T(8,128)} copy(f32[1,16,16,256]{3,2,1,0:T(8,128)} %bitcast.2) | data formatting | bytes 524288

commit v3 on v2

--- a/solution.py
+++ b/solution.py
@@ -101,10 +101,17 @@
 ):
     t, s = lax.axis_index("tm"), lax.axis_index("space")
     groups = T // GROUP
-    MAIN = T - GROUP
+    LAST = T - 3
+    MAIN = T - 2
     slot = lax.rem(t, GROUP)
-    home = t - slot
-    chain = slot == 0
+
+    def home_of(group):
+        return jnp.where(group == groups - 1, LAST, T - GROUP + 2 * group)
+
+    home = home_of((t - slot) // GROUP)
+    served = jnp.where(t == LAST, groups - 1, (t - (T - GROUP)) // 2)
+    chain = (t == LAST) | ((t >= T - GROUP) & (lax.rem(t, 2) == 0) & (served < groups - 1))
+    first = served * GROUP
     main = t == MAIN
 
     def beside(step):
@@ -118,7 +125,7 @@
     for step in (-1, 1):
         pl.when((s + step >= 0) & (s + step < S))(functools.partial(greet, t, s + step))
     pl.when(t < T - 1)(lambda: greet(t + 1, s))
-    pl.when(slot != 0)(lambda: greet(home, s))
+    pl.when(t != home)(lambda: greet(home, s))
     pl.when((t >= GROUP) & (t != MAIN))(lambda: greet(MAIN, s))
 
     @pl.when(chain)
@@ -130,7 +137,7 @@
     def _():
         for z in range(S):
             for x in range(groups - 1):
-                greet(x * GROUP, z)
+                greet(T - GROUP + 2 * x, z)
             pl.when(s != z)(functools.partial(greet, t, z))
 
     fields = ((q_in, lv.at[0]), (u_in, st.at[0]), (w_in, st.at[1]), (v_in, st.at[2]),
@@ -147,8 +154,8 @@
         return jnp.where(condition, one, zero)
 
     expected = flag(s > 0) + flag(s < S - 1) + flag(t > 0)
-    expected = expected + flag(chain) * (GROUP - 1 + flag(s > 1) + flag(s < S - 2))
-    expected = expected + flag(chain & (t != MAIN)) * S + flag(main) * (T - GROUP - 1 + S - 1)
+    expected = expected + flag(chain) * (GROUP + flag(s > 1) + flag(s < S - 2))
+    expected = expected + flag(chain & (t != LAST)) * S - flag(t == LAST) + flag(main) * (T - GROUP - 1 + S - 1)
     pl.semaphore_wait(barrier, expected)
 
     def halo(i, side):
@@ -186,8 +193,10 @@
 
     @pl.when(chain)
     def _():
-        for n in range(1, GROUP):
-            pl.semaphore_signal(go, inc=1, device_id=(home + n, s), device_id_type=MESH)
+        for n in range(GROUP):
+            @pl.when(first + n != t)
+            def _(n=n):
+                pl.semaphore_signal(go, inc=1, device_id=(first + n, s), device_id_type=MESH)
         for has, lo in ((s > 1, 0), (s > 0, CW), (s < S - 1, 3 * CW), (s < S - 2, 4 * CW)):
             @pl.when(jnp.logical_not(has))
             def _(lo=lo):
@@ -253,13 +262,16 @@
         return to_slab(cs_own, lambda lo: cs_win.at[:, pl.ds(lo, CW)],
                        c_send.at[j], c_recv.at[j], steps[j])
 
-    @pl.when(chain)
+    @pl.when(chain | main)
     def _():
         for i in range(5):
             sum_pairs(st.at[i], HF)
-            part = restrict(pairs[...])
-            cs_own[i] = part
-            cs_win[i, 2 * CW : 3 * CW] = part
+            cs_own[i] = restrict(pairs[...])
+
+    @pl.when(chain)
+    def _():
+        for i in range(5):
+            cs_win[i, 2 * CW : 3 * CW] = cs_own[i]
         for j in range(4):
             pl.when(there(steps[j]))(lambda j=j: cs_copy(j).start())
 
@@ -322,7 +334,7 @@
 
     sum_pairs(ends, 0)
     pl.when(t < T - 1)(lambda: start_copy.wait_recv())
-    pl.when(slot != 0)(lambda: pl.semaphore_wait(go, 1))
+    pl.when(t != home)(lambda: pl.semaphore_wait(go, 1))
 
     def r_copy(n, kind, j):
         step = (0,) + steps
@@ -337,35 +349,32 @@
 
     pieces = ((0, 1, 2, 3, 4), (0, 3, 4), (0, 3, 4), (0,))
 
-    def r_each(n, act, wait):
+    def r_each(act):
         for kind in range(TURNS):
-            @pl.when(lax.rem(n, TURNS) == kind)
+            @pl.when(lax.rem(slot, TURNS) == kind)
             def _(kind=kind):
-                r_pieces(n, kind, act, wait)
+                r_pieces(slot, kind, act, False)
 
     def r_pieces(n, kind, act, wait):
         for j in pieces[kind]:
             step = ((0,) + steps)[j]
-            own_slab = n != 0
-            condition = own_slab if step == 0 else there(-step if wait else step)
-            if condition is True:
-                act(r_copy(n, kind, j))
-            elif condition is not False:
-                pl.when(condition)(lambda j=j: act(r_copy(n, kind, j)))
+            other = (first + n != t) if wait else (home != t)
+            condition = other if step == 0 else there(-step if wait else step)
+            pl.when(condition)(lambda j=j: act(r_copy(n, kind, j)))
 
     @pl.when(t < T - 1)
     def _():
         r_own[...] = restrict(pairs[...]) - s_next[...]
 
-        @pl.when(chain)
+        @pl.when(t == home)
         def _():
-            r_win[0, 2 * CW : 3 * CW] = r_own[...]
-        r_each(slot, lambda copy: copy.start(), False)
+            r_win[LAST % GROUP, 2 * CW : 3 * CW] = r_own[...]
+        r_each(lambda copy: copy.start())
 
     def d_copy(n):
         return pltpu.make_async_remote_copy(
             src_ref=d_out.at[n], dst_ref=d_in, send_sem=d_send.at[n], recv_sem=d_recv,
-            device_id=(home + n, s), device_id_type=MESH)
+            device_id=(first + n, s), device_id_type=MESH)
 
     def e_copy(j):
         return to_slab(e_win.at[pl.ds(2 * CW, CW)], lambda lo: e_win.at[pl.ds(lo, CW)],
@@ -373,8 +382,8 @@
 
     def p_copy(z):
         return pltpu.make_async_remote_copy(
-            src_ref=p_own, dst_ref=p_full.at[home // GROUP, pl.ds(s * CW, CW)],
-            send_sem=p_send.at[z], recv_sem=p_recv.at[home // GROUP, s],
+            src_ref=p_own, dst_ref=p_full.at[served, pl.ds(s * CW, CW)],
+            send_sem=p_send.at[z], recv_sem=p_recv.at[served, s],
             device_id=(MAIN, z), device_id_type=MESH)
 
     def p_arrival(x, z):
@@ -392,10 +401,14 @@
             src = wb.at[1 - j % 2]
         own_lo, own_hi = 2 * CW, 3 * CW
         d_out[n] = stencil(ccoef, src, own_lo, CW)
-        d_copy(n).start()
+        pl.when(first + n != t)(lambda: d_copy(n).start())
+
+        @pl.when(first + n == t)
+        def _():
+            d_in[...] = d_out[n]
 
         if n == GROUP - 1:
-            @pl.when(t != MAIN)
+            @pl.when(t != LAST)
             def _():
                 r_pieces(n, kind, lambda copy: copy.wait_recv(), True)
                 p_own[...] = d_out[n] + r_win[n, own_lo:own_hi]
@@ -460,7 +473,7 @@
             return carry
         lax.fori_loop(0, T - GROUP, big_turn, 0)
 
-    pl.when(slot > 0)(lambda: d_copy(slot).wait_recv())
+    pl.when((slot > 0) & (t != LAST))(lambda: d_copy(slot).wait_recv())
     pl.when((t >= GROUP) & (t != MAIN))(lambda: g_copy(t - GROUP).wait_recv())
 
     @pl.when(main)
@@ -485,7 +498,7 @@
             pl.when(has_target[side])(lambda i=i, side=side: halo(i, side).wait_send())
         pl.when(has_target[side])(lambda side=side: halo2(side).wait_send())
     pl.when(t > 0)(lambda: start_copy.wait_send())
-    pl.when(t < T - 1)(lambda: r_each(slot, lambda copy: copy.wait_send(), False))
+    pl.when(t < T - 1)(lambda: r_each(lambda copy: copy.wait_send()))
 
     @pl.when(chain)
     def _():
@@ -494,9 +507,9 @@
 
             pl.when(there(steps[j]))(lambda j=j: e_copy(j).wait_send())
         for n in range(1, GROUP):
-            d_copy(n).wait_send()
-
-        @pl.when(t != MAIN)
+            pl.when(first + n != t)(lambda n=n: d_copy(n).wait_send())
+
+        @pl.when(t != LAST)
         def _():
             for z in range(S):
                 p_copy(z).wait_send()

time: 67.8 us -> 60.6 us (0.89); the launches traced: 66.5 us -> 60.5 us
  Pallas kernels: 64.9 us -> 58.8 us
    pallas_call x1, Pallas kernels: 64.9 us -> 58.8 us  [shards(): pl.pallas_call(functools.partial(kernel, T, S), out_shape=jax.ShapeDtypeS...]
where the time goes in v3:
time: 60.6 us; the launch traced here: 60.5 us
  Pallas kernels  58.8 us (97%)
  local copies, waits for them, and re-layouts  1.67 us (3%)
    pallas_call x1, Pallas kernels, shards(): pl.pallas_call(functools.partial(kernel, T, S), out_shape=jax.ShapeDtypeS...  58.8 us
    unnamed x1, local copies, waits for them, and re-layouts  1.67 us

profile of v3, /device:TPU:23, one launch (start us, length us, event | category | flops | bytes accessed | tf_op | source)
XLA Modules:
  0.0 60.5 jit_solution(5001124183937220312)
XLA Ops:
  0.0 58.8 %shard_map.73 = f32[16,16,256]{2,1,0:T(8,128)} custom-call(f32[16,16,256]{2,1,0:T(8,128)} %bitcast.3, f32[16,16,256]{2,1,0:T(8,128)} %u_in.1, f32[16,16,256]{2,1,0:T(8,128)} %w_in.1, f32[16,16,256]{2,1,0:T(8,128)} %v_in.1, s32[16,16,256]{2,1,0:T(8,128)} %cls_in.1, s32[16,16,256]{2,1,0:T(8,128)} %msk_in.1, f32[8]{0:T(128)} %kd.1), custom_call_target="tpu_custom_call" | custom-call | tf_op jit(solution)/shard_map/pallas_call | solution.py:534
  58.8 1.7 %copy.9 = f32[1,16,16,256]{3,2,1,0:T(8,128)} copy(f32[1,16,16,256]{3,2,1,0:T(8,128)} %bitcast.2) | data formatting | bytes 524288

commit v4 on v3

--- a/solution.py
+++ b/solution.py
@@ -14,6 +14,7 @@
 WIN = 5 * CW
 TURNS = 4
 GROUP = 2 * TURNS
+HALF = TURNS
 F32 = jnp.float32
 
 
@@ -95,24 +96,37 @@
     st, ints, lv, coef, ends, pairs, s_own, s_next, r_own,
     cs_own, cs_win, ccoef, r_win, e_win, wb, d_out, d_in,
     cs_full, fcoef, p_own, p_full, cur, g_out, g_in,
-    loc_sem, h_send, h_recv, h2_send, h2_recv, s_sem, r_send, r_recv,
+    loc_sem, h_send, h_recv, m_send, m_recv, h2_send, h2_recv, s_sem, r_send, r_recv,
     c_send, c_recv, e_send, e_recv, d_send, d_recv,
     f_send, f_recv, p_send, p_recv, g_send, g_recv, go,
 ):
     t, s = lax.axis_index("tm"), lax.axis_index("space")
-    groups = T // GROUP
-    LAST = T - 3
+    groups = T // GROUP + 1
+    LAST = T - 9
     MAIN = T - 2
-    slot = lax.rem(t, GROUP)
-
-    def home_of(group):
-        return jnp.where(group == groups - 1, LAST, T - GROUP + 2 * group)
-
-    home = home_of((t - slot) // GROUP)
-    served = jnp.where(t == LAST, groups - 1, (t - (T - GROUP)) // 2)
-    chain = (t == LAST) | ((t >= T - GROUP) & (lax.rem(t, 2) == 0) & (served < groups - 1))
-    first = served * GROUP
+    homes = [T - 8, T - 6, T - 4, T - 11][: groups - 1] + [LAST]
+    slot = jnp.where(t < HALF, t + HALF, lax.rem(t, GROUP))
+    group = jnp.where(t < HALF, 0, t // GROUP + 1)
+
+    def among(pairs, other):
+        value = jnp.int32(other)
+        for condition, choice in pairs:
+            value = jnp.where(condition, jnp.int32(choice), value)
+        return value
+
+    home = among([(group == g, row) for g, row in enumerate(homes)], 0)
+    served = among([(t == row, g) for g, row in enumerate(homes)], -1)
+    chain = served >= 0
+    final = served == groups - 1
+    first = jnp.where(served == 0, -HALF, (served - 1) * GROUP)
+    short = served < 2
     main = t == MAIN
+    helper = t == T - 10
+    core = lax.rem(t, 2)
+    mate = t + 1 - 2 * core
+
+    def member(n):
+        return jnp.logical_not(short) if n < HALF else served >= 0
 
     def beside(step):
         return lax.rem(s + step + S, S)
@@ -125,8 +139,9 @@
     for step in (-1, 1):
         pl.when((s + step >= 0) & (s + step < S))(functools.partial(greet, t, s + step))
     pl.when(t < T - 1)(lambda: greet(t + 1, s))
+    greet(mate, s)
     pl.when(t != home)(lambda: greet(home, s))
-    pl.when((t >= GROUP) & (t != MAIN))(lambda: greet(MAIN, s))
+    pl.when((t >= HALF) & (t != MAIN))(lambda: greet(MAIN, s))
 
     @pl.when(chain)
     def _():
@@ -136,8 +151,8 @@
     @pl.when(main)
     def _():
         for z in range(S):
-            for x in range(groups - 1):
-                greet(T - GROUP + 2 * x, z)
+            for row in homes[:-1] + [T - 10]:
+                greet(row, z)
             pl.when(s != z)(functools.partial(greet, t, z))
 
     fields = ((q_in, lv.at[0]), (u_in, st.at[0]), (w_in, st.at[1]), (v_in, st.at[2]),
@@ -153,18 +168,29 @@
     def flag(condition):
         return jnp.where(condition, one, zero)
 
-    expected = flag(s > 0) + flag(s < S - 1) + flag(t > 0)
-    expected = expected + flag(chain) * (GROUP + flag(s > 1) + flag(s < S - 2))
-    expected = expected + flag(chain & (t != LAST)) * S - flag(t == LAST) + flag(main) * (T - GROUP - 1 + S - 1)
+    expected = 1 + flag(s > 0) + flag(s < S - 1) + flag(t > 0)
+    expected = expected + flag(chain) * (flag(s > 1) + flag(s < S - 2))
+    expected = expected + flag(chain) * (GROUP - HALF * flag(short)) - flag(chain & (home == t))
+    expected = expected + flag(chain & (t != LAST)) * S + flag(helper) * S + flag(main) * (T - HALF - 1 + S - 1)
     pl.semaphore_wait(barrier, expected)
+
+    PART = HF // 2
 
     def halo(i, side):
         src, dst = fields[i]
         src_lo, dst_lo = ((0, HF + W), (W - HF, 0))[side]
-        return pltpu.make_async_remote_copy(
-            src_ref=src.at[pl.ds(src_lo, HF)], dst_ref=dst.at[pl.ds(dst_lo, HF)],
+        n, skip = (HF, 0) if i == 0 else (PART, core * PART)
+        return pltpu.make_async_remote_copy(
+            src_ref=src.at[pl.ds(src_lo + skip, n)], dst_ref=dst.at[pl.ds(dst_lo + skip, n)],
             send_sem=h_send.at[i, side], recv_sem=h_recv.at[i, side],
             device_id=(t, beside(2 * side - 1)), device_id_type=MESH)
+
+    def share(i, side, which):
+        dst = fields[i][1]
+        part = dst.at[pl.ds((HF + W, 0)[side] + which * PART, PART)]
+        return pltpu.make_async_remote_copy(
+            src_ref=part, dst_ref=part, send_sem=m_send.at[i, side], recv_sem=m_recv.at[i, side],
+            device_id=(mate, s), device_id_type=MESH)
 
     def halo2(side):
         src_lo, dst_lo = ((HF, HF + W), (W, 0))[side]
@@ -194,7 +220,7 @@
     @pl.when(chain)
     def _():
         for n in range(GROUP):
-            @pl.when(first + n != t)
+            @pl.when(member(n) & (first + n != t))
             def _(n=n):
                 pl.semaphore_signal(go, inc=1, device_id=(first + n, s), device_id_type=MESH)
         for has, lo in ((s > 1, 0), (s > 0, CW), (s < S - 1, 3 * CW), (s < S - 2, 4 * CW)):
@@ -262,7 +288,7 @@
         return to_slab(cs_own, lambda lo: cs_win.at[:, pl.ds(lo, CW)],
                        c_send.at[j], c_recv.at[j], steps[j])
 
-    @pl.when(chain | main)
+    @pl.when(chain | main | helper)
     def _():
         for i in range(5):
             sum_pairs(st.at[i], HF)
@@ -286,6 +312,15 @@
             src_ref=cs_own, dst_ref=cs_full.at[:, pl.ds(1 + z * CW, CW)],
             send_sem=f_send.at[z], recv_sem=f_recv.at[z],
             device_id=(MAIN, z), device_id_type=MESH)
+
+    def f_each(who, act):
+        for z in range(S):
+            gap = lax.rem(z - s + S, S)
+            near = (gap <= 2) | (gap >= S - 2)
+            wanted = jnp.logical_not(near) if who is helper else near & (gap != 0)
+            pl.when(who & wanted)(lambda z=z: act(z))
+
+    f_each(helper, lambda z: f_copy(z).start())
 
     @pl.when(main)
     def _():
@@ -311,7 +346,15 @@
     inner(0)
     for i in order:
         for side in (0, 1):
-            pl.when(has_target[1 - side])(lambda i=i, side=side: halo(i, side).wait_recv())
+            @pl.when(has_target[1 - side])
+            def _(i=i, side=side):
+                halo(i, side).wait_recv()
+                if i > 0:
+                    share(i, side, core).start()
+    for i in order[:-1]:
+        for side in (0, 1):
+            pl.when(has_target[1 - side])(
+                lambda i=i, side=side: share(i, side, 1 - core).wait_recv())
     for lo in (0, HF + W):
         for i, n in chunks(lo, lo + HF, 2):
             widen(i, n)
@@ -322,11 +365,7 @@
     for side in (0, 1):
         pl.when(has_target[side])(lambda side=side: halo2(side).start())
 
-    @pl.when(main)
-    def _():
-        for z in range(S):
-            pl.when(s != z)(lambda z=z: f_copy(z).start())
-
+    f_each(main, lambda z: f_copy(z).start())
     inner(HF)
     for side in (0, 1):
         pl.when(has_target[1 - side])(lambda side=side: halo2(side).wait_recv())
@@ -368,7 +407,7 @@
 
         @pl.when(t == home)
         def _():
-            r_win[LAST % GROUP, 2 * CW : 3 * CW] = r_own[...]
+            r_win[slot, 2 * CW : 3 * CW] = r_own[...]
         r_each(lambda copy: copy.start())
 
     def d_copy(n):
@@ -407,16 +446,19 @@
         def _():
             d_in[...] = d_out[n]
 
+        def arrivals():
+            r_pieces(n, kind, lambda copy: copy.wait_recv(), True)
+
         if n == GROUP - 1:
-            @pl.when(t != LAST)
+            @pl.when(jnp.logical_not(final))
             def _():
-                r_pieces(n, kind, lambda copy: copy.wait_recv(), True)
+                arrivals()
                 p_own[...] = d_out[n] + r_win[n, own_lo:own_hi]
                 for z in range(S):
                     p_copy(z).start()
             return
-        r_pieces(n, kind, lambda copy: copy.wait_recv(), True)
         into = slice(own_lo, own_hi)
+        arrivals()
         dst[into] = d_out[n] + r_win[n, into]
         for i, m in chunks(lo + 4, own_lo, CW) + chunks(own_hi, hi - 4, CW):
             dst[i : i + m] = stencil(ccoef, src, i, m) + r_win[n, i : i + m]
@@ -429,24 +471,32 @@
         for lo, n in chunks(1, WIN - 1, 4):
             make_coefs(cstat, ccoef, lo, n, 0.5)
 
-        r_pieces(0, 0, lambda copy: copy.wait_recv(), True)
-        src = r_win.at[0]
-        for n in range(1, TURNS):
-            turn(n, src, wb.at[1] if n < TURNS - 1 else e_win)
-            src = wb.at[1]
-        for j in range(4):
-            pl.when(there(steps[j]))(lambda j=j: e_copy(j).start())
-        for j in range(4):
-            pl.when(there(-steps[j]))(lambda j=j: e_copy(j).wait_recv())
-        src = e_win
-        for n in range(TURNS, GROUP):
-            turn(n, src, wb.at[1])
-            src = wb.at[1]
+        @pl.when(jnp.logical_not(short))
+        def _():
+            r_pieces(0, 0, lambda copy: copy.wait_recv(), True)
+            src = r_win.at[0]
+            for n in range(1, HALF):
+                turn(n, src, wb.at[1] if n < HALF - 1 else e_win)
+                src = wb.at[1]
+            for j in range(4):
+                pl.when(there(steps[j]))(lambda j=j: e_copy(j).start())
+            for j in range(4):
+                pl.when(there(-steps[j]))(lambda j=j: e_copy(j).wait_recv())
+            turn(HALF, e_win, wb.at[1])
+
+        @pl.when(short)
+        def _():
+            r_pieces(HALF, 0, lambda copy: copy.wait_recv(), True)
+            for i, m in chunks(4, WIN - 4, CW):
+                wb[1, i : i + m] = r_win[HALF, i : i + m]
+
+        for n in range(HALF + 1, GROUP):
+            turn(n, wb.at[1], wb.at[1])
 
     def g_copy(m):
         return pltpu.make_async_remote_copy(
             src_ref=g_out.at[m], dst_ref=g_in, send_sem=g_send.at[m], recv_sem=g_recv,
-            device_id=(m + GROUP, s), device_id_type=MESH)
+            device_id=(m + HALF, s), device_id_type=MESH)
 
     @pl.when(main)
     def _():
@@ -457,9 +507,9 @@
             make_coefs(fstat, fcoef, lo, n, 0.5)
 
         def big_turn(m, carry):
-            @pl.when(lax.rem(m, GROUP) == 0)
+            @pl.when((m == 0) | (lax.rem(m, GROUP) == HALF))
             def _():
-                x = m // GROUP
+                x = (m + HALF) // GROUP
                 for z in range(S):
                     p_arrival(x, z).wait_recv()
                 for i, n in chunks(0, S * CW, CW):
@@ -469,22 +519,23 @@
                 for i, n in chunks(1, S * CW + 1, CW):
                     cur[b, i : i + n] = stencil(fcoef, cur.at[a], i, n)
             g_out[m] = cur[0, pl.ds(1 + s * CW, CW)]
-            pl.when(m + GROUP != MAIN)(lambda: g_copy(m).start())
+            pl.when(m + HALF != MAIN)(lambda: g_copy(m).start())
             return carry
-        lax.fori_loop(0, T - GROUP, big_turn, 0)
-
-    pl.when((slot > 0) & (t != LAST))(lambda: d_copy(slot).wait_recv())
-    pl.when((t >= GROUP) & (t != MAIN))(lambda: g_copy(t - GROUP).wait_recv())
+        lax.fori_loop(0, T - HALF, big_turn, 0)
+
+    start = (t == 0) | (t == HALF) | (slot == 0)
+    pl.when(jnp.logical_not(start) & (t != home))(lambda: d_copy(slot).wait_recv())
+    pl.when((t >= HALF) & (t != MAIN))(lambda: g_copy(t - HALF).wait_recv())
 
     @pl.when(main)
     def _():
-        g_in[...] = g_out[MAIN - GROUP]
-
-    @pl.when(slot == 0)
+        g_in[...] = g_out[MAIN - HALF]
+
+    @pl.when(start)
     def _():
         d_in[...] = jnp.zeros((CW, CZ, CY), F32)
 
-    @pl.when(t >= GROUP)
+    @pl.when(t >= HALF)
     def _():
         d_in[...] = d_in[...] + g_in[...]
 
@@ -496,6 +547,9 @@
     for side in (0, 1):
         for i in order:
             pl.when(has_target[side])(lambda i=i, side=side: halo(i, side).wait_send())
+            if i > 0:
+                pl.when(has_target[1 - side])(
+                    lambda i=i, side=side: share(i, side, core).wait_send())
         pl.when(has_target[side])(lambda side=side: halo2(side).wait_send())
     pl.when(t > 0)(lambda: start_copy.wait_send())
     pl.when(t < T - 1)(lambda: r_each(lambda copy: copy.wait_send()))
@@ -505,29 +559,31 @@
         for j in range(4):
             pl.when(there(steps[j]))(lambda j=j: cs_copy(j).wait_send())
 
-            pl.when(there(steps[j]))(lambda j=j: e_copy(j).wait_send())
+            pl.when(there(steps[j]) & jnp.logical_not(short))(
+                lambda j=j: e_copy(j).wait_send())
         for n in range(1, GROUP):
-            pl.when(first + n != t)(lambda n=n: d_copy(n).wait_send())
+            begun = jnp.logical_not(short) if n <= HALF else chain
+            pl.when(begun & (first + n != t))(lambda n=n: d_copy(n).wait_send())
 
         @pl.when(t != LAST)
         def _():
             for z in range(S):
                 p_copy(z).wait_send()
 
+    f_each(helper, lambda z: f_copy(z).wait_send())
+    f_each(main, lambda z: f_copy(z).wait_send())
+
     @pl.when(main)
     def _():
-        for z in range(S):
-            pl.when(s != z)(lambda z=z: f_copy(z).wait_send())
-
         def drain(m, carry):
-            pl.when(m + GROUP != MAIN)(lambda: g_copy(m).wait_send())
+            pl.when(m + HALF != MAIN)(lambda: g_copy(m).wait_send())
             return carry
-        lax.fori_loop(0, T - GROUP, drain, 0)
+        lax.fori_loop(0, T - HALF, drain, 0)
 
 
 def shards(starts, u, w, v, cls, msk, kd):
     T, S = lax.axis_size("tm"), lax.axis_size("space")
-    groups = T // GROUP
+    groups = T // GROUP + 1
     dma = pltpu.SemaphoreType.DMA
     anywhere = pl.BlockSpec(memory_space=pl.ANY)
     slab = (CW, CZ, CY)
@@ -559,9 +615,10 @@
             pltpu.VMEM(slab, F32),
             pltpu.VMEM((groups - 1, S * CW, CZ, CY), F32),
             pltpu.VMEM((3, S * CW + 2, CZ, CY), F32),
-            pltpu.VMEM((T - GROUP,) + slab, F32),
+            pltpu.VMEM((T - HALF,) + slab, F32),
             pltpu.VMEM(slab, F32),
             dma((6,)),
+            dma((6, 2)), dma((6, 2)),
             dma((6, 2)), dma((6, 2)),
             dma((2,)), dma((2,)),
             dma((2,)),
@@ -571,7 +628,7 @@
             dma((GROUP,)), dma(()),
             dma((S,)), dma((S,)),
             dma((S,)), dma((groups - 1, S)),
-            dma((T - GROUP,)), dma(()),
+            dma((T - HALF,)), dma(()),
             pltpu.SemaphoreType.REGULAR,
         ],
         compiler_params=pltpu.CompilerParams(

time: 60.6 us -> 56.4 us (0.931)
  Pallas kernels: 58.8 us -> 54.6 us
    pallas_call x1, Pallas kernels: 58.8 us -> 54.6 us  [shards(): pl.pallas_call(functools.partial(kernel, T, S), out_shape=jax.ShapeDtypeS...]
where the time goes in v4:
time: 56.4 us; the launch traced here: 56.2 us
  Pallas kernels  54.6 us (97%)
  local copies, waits for them, and re-layouts  1.67 us (3%)
    pallas_call x1, Pallas kernels, shards(): pl.pallas_call(functools.partial(kernel, T, S), out_shape=jax.ShapeDtypeS...  54.6 us
    unnamed x1, local copies, waits for them, and re-layouts  1.67 us

profile of v4, /device:TPU:23, one launch (start us, length us, event | category | flops | bytes accessed | tf_op | source)
XLA Modules:
  0.0 56.2 jit_solution(7900867404424788115)
XLA Ops:
  0.0 54.6 %shard_map.73 = f32[16,16,256]{2,1,0:T(8,128)} custom-call(f32[16,16,256]{2,1,0:T(8,128)} %bitcast.3, f32[16,16,256]{2,1,0:T(8,128)} %u_in.1, f32[16,16,256]{2,1,0:T(8,128)} %w_in.1, f32[16,16,256]{2,1,0:T(8,128)} %v_in.1, s32[16,16,256]{2,1,0:T(8,128)} %cls_in.1, s32[16,16,256]{2,1,0:T(8,128)} %msk_in.1, f32[8]{0:T(128)} %kd.1), custom_call_target="tpu_custom_call" | custom-call | tf_op jit(solution)/shard_map/pallas_call | solution.py:590
  54.6 1.7 %copy.9 = f32[1,16,16,256]{3,2,1,0:T(8,128)} copy(f32[1,16,16,256]{3,2,1,0:T(8,128)} %bitcast.2) | data formatting | bytes 524288

commit v5 on v4

--- a/solution.py
+++ b/solution.py
@@ -92,7 +92,7 @@
 def kernel(
     T, S,
     q_in, u_in, w_in, v_in, cls_in, msk_in, kd,
-    out,
+    ends_out, delta_out,
     st, ints, lv, coef, ends, pairs, s_own, s_next, r_own,
     cs_own, cs_win, ccoef, r_win, e_win, wb, d_out, d_in,
     cs_full, fcoef, p_own, p_full, cur, g_out, g_in,
@@ -200,6 +200,7 @@
             device_id=(t, beside(2 * side - 1)), device_id_type=MESH)
 
     has_target = (s > 0, s < S - 1)
+    far_first = sorted(range(S), key=lambda z: -min(z, S - z))
     order = (1, 2, 3, 4, 5, 0)
     for i in order:
         for side in (0, 1):
@@ -234,6 +235,12 @@
                     r_win[n, lo : lo + CW] = blank
                 e_win[lo : lo + CW] = blank
 
+    @pl.when(chain & short)
+    def _():
+        for lo in (0, WIN - CW // 2):
+            for i in range(5):
+                cs_win[i, lo : lo + CW // 2] = jnp.zeros((CW // 2, CZ, CY), F32)
+
     @pl.when(main)
     def _():
         margin = jnp.zeros((1, CZ, CY), F32)
@@ -271,8 +278,6 @@
     stat = [st.at[i] for i in range(5)]
     for lo, n in chunks(HF, HF + W, 2):
         widen(lo, n)
-    for lo, n in chunks(HF + 1, HF + W - 1, 2):
-        make_coefs(stat, coef, lo, n, 1.0)
 
     def to_slab(src, dst_of, send, recv, step):
         return pltpu.make_async_remote_copy(
@@ -288,6 +293,20 @@
         return to_slab(cs_own, lambda lo: cs_win.at[:, pl.ds(lo, CW)],
                        c_send.at[j], c_recv.at[j], steps[j])
 
+    def cs_half(j):
+        lo = CW // 2 if steps[j] > 0 else 0
+        return to_slab(cs_own.at[:, pl.ds(lo, CW // 2)],
+                       lambda base: cs_win.at[:, pl.ds(base + lo, CW // 2)],
+                       c_send.at[j], c_recv.at[j], steps[j])
+
+    def cs_each(sending, act):
+        for j in range(4):
+            way = there(steps[j] if sending else -steps[j])
+            if j < 2:
+                pl.when(way & short)(lambda j=j: act(cs_half(j)))
+                way = way & jnp.logical_not(short)
+            pl.when(way)(lambda j=j: act(cs_copy(j)))
+
     @pl.when(chain | main | helper)
     def _():
         for i in range(5):
@@ -298,8 +317,10 @@
     def _():
         for i in range(5):
             cs_win[i, 2 * CW : 3 * CW] = cs_own[i]
-        for j in range(4):
-            pl.when(there(steps[j]))(lambda j=j: cs_copy(j).start())
+        cs_each(True, lambda copy: copy.start())
+
+    for lo, n in chunks(HF + 1, HF + W - 1, 2):
+        make_coefs(stat, coef, lo, n, 1.0)
 
     def f_copy(z):
         return pltpu.make_async_remote_copy(
@@ -367,10 +388,19 @@
 
     f_each(main, lambda z: f_copy(z).start())
     inner(HF)
+
+    @pl.when(chain)
+    def _():
+        cs_each(False, lambda copy: copy.wait_recv())
+        cstat = [cs_win.at[i] for i in range(5)]
+        for lo, n in chunks(1, WIN - 1, 4):
+            make_coefs(cstat, ccoef, lo, n, 0.5)
+
     for side in (0, 1):
         pl.when(has_target[1 - side])(lambda side=side: halo2(side).wait_recv())
     outer(HF)
 
+    pltpu.make_async_copy(ends, ends_out, loc_sem.at[0]).start()
     sum_pairs(ends, 0)
     pl.when(t < T - 1)(lambda: start_copy.wait_recv())
     pl.when(t != home)(lambda: pl.semaphore_wait(go, 1))
@@ -386,7 +416,7 @@
             send_sem=r_send.at[j], recv_sem=r_recv.at[n, j],
             device_id=(home, beside(step)), device_id_type=MESH)
 
-    pieces = ((0, 1, 2, 3, 4), (0, 3, 4), (0, 3, 4), (0,))
+    pieces = ((1, 2, 3, 4, 0), (3, 4, 0), (3, 4, 0), (0,))
 
     def r_each(act):
         for kind in range(TURNS):
@@ -454,8 +484,8 @@
             def _():
                 arrivals()
                 p_own[...] = d_out[n] + r_win[n, own_lo:own_hi]
-                for z in range(S):
-                    p_copy(z).start()
+                for z in far_first:
+                    p_copy(lax.rem(s + z, S)).start()
             return
         into = slice(own_lo, own_hi)
         arrivals()
@@ -465,12 +495,6 @@
 
     @pl.when(chain)
     def _():
-        for j in range(4):
-            pl.when(there(-steps[j]))(lambda j=j: cs_copy(j).wait_recv())
-        cstat = [cs_win.at[i] for i in range(5)]
-        for lo, n in chunks(1, WIN - 1, 4):
-            make_coefs(cstat, ccoef, lo, n, 0.5)
-
         @pl.when(jnp.logical_not(short))
         def _():
             r_pieces(0, 0, lambda copy: copy.wait_recv(), True)
@@ -539,10 +563,8 @@
     def _():
         d_in[...] = d_in[...] + g_in[...]
 
-    fine_delta = prolong(d_in[...])
-    for i in range(CW):
-        out[2 * i] = ends[2 * i] + fine_delta[i]
-        out[2 * i + 1] = ends[2 * i + 1] + fine_delta[i]
+    delta_out[...] = d_in[...]
+    pltpu.make_async_copy(ends, ends_out, loc_sem.at[0]).wait()
 
     for side in (0, 1):
         for i in order:
@@ -557,10 +579,10 @@
     @pl.when(chain)
     def _():
         for j in range(4):
-            pl.when(there(steps[j]))(lambda j=j: cs_copy(j).wait_send())
 
             pl.when(there(steps[j]) & jnp.logical_not(short))(
                 lambda j=j: e_copy(j).wait_send())
+        cs_each(True, lambda copy: copy.wait_send())
         for n in range(1, GROUP):
             begun = jnp.logical_not(short) if n <= HALF else chain
             pl.when(begun & (first + n != t))(lambda n=n: d_copy(n).wait_send())
@@ -579,6 +601,13 @@
             pl.when(m + HALF != MAIN)(lambda: g_copy(m).wait_send())
             return carry
         lax.fori_loop(0, T - HALF, drain, 0)
+
+
+def correct(ends, delta, out):
+    fine_delta = prolong(delta[...])
+    for i in range(CW):
+        out[2 * i] = ends[2 * i] + fine_delta[i]
+        out[2 * i + 1] = ends[2 * i + 1] + fine_delta[i]
 
 
 def shards(starts, u, w, v, cls, msk, kd):
@@ -587,11 +616,11 @@
     dma = pltpu.SemaphoreType.DMA
     anywhere = pl.BlockSpec(memory_space=pl.ANY)
     slab = (CW, CZ, CY)
-    result = pl.pallas_call(
+    ends, delta = pl.pallas_call(
         functools.partial(kernel, T, S),
-        out_shape=jax.ShapeDtypeStruct((W, Z, Y), F32),
+        out_shape=(jax.ShapeDtypeStruct((W, Z, Y), F32), jax.ShapeDtypeStruct(slab, F32)),
         in_specs=[anywhere] * 6 + [pl.BlockSpec(memory_space=pltpu.SMEM)],
-        out_specs=pl.BlockSpec(memory_space=pltpu.VMEM),
+        out_specs=(anywhere, pl.BlockSpec(memory_space=pltpu.VMEM)),
         scratch_shapes=[
             pltpu.VMEM((5, E, Z, Y), F32),
             pltpu.VMEM((2, E, Z, Y), jnp.int32),
@@ -634,6 +663,10 @@
         compiler_params=pltpu.CompilerParams(
             collective_id=0, has_side_effects=True, vmem_limit_bytes=56 * 1024 * 1024),
     )(starts[0], u, w, v, cls, msk, kd)
+    vmem = pl.BlockSpec(memory_space=pltpu.VMEM)
+    result = pl.pallas_call(
+        correct, out_shape=jax.ShapeDtypeStruct((W, Z, Y), F32),
+        in_specs=[vmem, vmem], out_specs=vmem)(ends, delta)
     return result[None]
 
 

time: 56.4 us -> 56.2 us (level)
  local copies, waits for them, and re-layouts: 1.67 us -> 0 us
  Pallas kernels: 54.6 us -> 56.1 us
    unnamed x1 -> x0, local copies, waits for them, and re-layouts: 1.67 us -> none
    pallas_call x1 -> x2, Pallas kernels: 54.6 us -> 56.1 us  [the longest x1 53.9 us: shards(): pl.pallas_call(functools.partial(kernel, T, S), out_shape=(jax.ShapeDtype...]
where the time goes in v5:
time: 56.2 us; the launch traced here: 56.1 us
  Pallas kernels  56.1 us (100%)
    pallas_call x1, Pallas kernels, shards(): pl.pallas_call(functools.partial(kernel, T, S), out_shape=(jax.ShapeDtype...  53.9 us
    pallas_call x1, Pallas kernels, shards(): pl.pallas_call(correct, out_shape=jax.ShapeDtypeStruct((W, Z, Y), F32), i...  2.19 us

profile of v5, /device:TPU:23, one launch (start us, length us, event | category | flops | bytes accessed | tf_op | source)
XLA Modules:
  0.0 56.1 jit_solution(17683334964318829462)
XLA Ops:
  0.0 53.9 %shard_map.73 = (f32[16,16,256]{2,1,0:T(8,128)}, f32[8,8,128]{2,1,0:T(8,128)}) custom-call(f32[16,16,256]{2,1,0:T(8,128)} %bitcast.2, f32[16,16,256]{2,1,0:T(8,128)} %u_in.1, f32[16,16,256]{2,1,0:T(8,128)} %w_in.1, f32[16,16,256]{2,1,0:T(8,128)} %v_in.1, s32[16,16,256]{2,1,0:T(8,128)} %cls_in.1, s32[16,16,256]{2,1,0:T(8,128)} %msk_in.1, f32[8]{0:T(128)} %kd.1), custom_call_target="tpu_custom_call" | custom-call | tf_op jit(solution)/shard_map/pallas_call | solution.py:619
  53.9 2.2 %shard_map.74 = f32[16,16,256]{2,1,0:T(8,128)} custom-call(f32[16,16,256]{2,1,0:T(8,128)} %get-tuple-element.7.ends, f32[8,8,128]{2,1,0:T(8,128)} %get-tuple-element.8.delta), custom_call_target="tpu_custom_call" | custom-call | tf_op jit(solution)/shard_map/pallas_call | solution.py:667
